TPU v7x, 256 devices: a whole 4x4x8 slice. The times are simulated.
256 devices in a mesh: elem: 256 (over z, y, x, core).
Axes of the slice: x: 4, y: 4, z: 8, core: 2. Of those that a mesh axis runs over, the one named last changes fastest.
Arguments:
- moment_fields: float32 [3, 512, 32768], P(None, None, 'elem'), may hold values from -6 to 6
- adjoint_fields: float32 [3, 512, 32768], P(None, None, 'elem'), may hold values from -6 to 6
- velocity: float32 [3, 512, 32768], P(None, None, 'elem'), may hold values from -12 to 12
- mass_weights: float32 [512, 32768], P(None, 'elem'), may hold values from 0.5 to 2
- diffusivity: float32 [3], replicated, may hold values from 0.1 to 0.5
- numbering: int32 [32768], P('elem'), may hold values from 0 to 32767, as said below
Outputs:
- moments: float32 [3, 512, 32768], P(None, None, 'elem')
- sensitivities: float32 [3, 512, 32768], P(None, None, 'elem')
Inputs may be any that keep to these rules, and one draw needn't show every extreme that they name: `numbering`: rows d * 128 to (d + 1) * 128 - 1 hold, in some order, each of the numbers c * 128 to (c + 1) * 128 - 1 once, where c = (d + 32) % 256.
All inputs are finite; a program needn't handle non-finite values.
Results may differ from a plain program's by a relative error of at most 0.0001.
Values sent between devices are 32-bit elements; how exact they have to be, the bound alone decides.
A program may use at most 64 MiB of HBM per device.

v0:
```python
import jax
import jax.numpy as jnp
import numpy as np
from jax import lax
from jax.sharding import PartitionSpec as P

DA = 4


time_step = 0.001
highest = lax.Precision.HIGHEST


def extended(cells, sides, width):
    for axis, dim in sides:
        count = lax.axis_size(axis)
        head = lax.slice_in_dim(cells, 0, width, axis=dim)
        tail = lax.slice_in_dim(cells, cells.shape[dim] - width, cells.shape[dim], axis=dim)
        cells = jnp.concatenate(
            [
                lax.ppermute(tail, axis, [(i, (i + 1) % count) for i in range(count)]),
                cells,
                lax.ppermute(head, axis, [((i + 1) % count, i) for i in range(count)]),
            ],
            axis=dim,
        )
    return cells


def from_behind(block, axis, distance):
    devices = range(lax.axis_size(axis))
    route = [((i - distance) % len(devices), i) for i in devices]
    return lax.ppermute(block, axis, route)


def gll_tables():
    points = [
        -1.0,
        -0.8717401485096066,
        -0.5917001814331423,
        -0.2092992179024789,
        0.2092992179024789,
        0.5917001814331423,
        0.8717401485096066,
        1.0,
    ]
    weights = [
        0.03571428571428571,
        0.21070422714350603,
        0.3411226924835044,
        0.4124587946587038,
        0.4124587946587038,
        0.3411226924835044,
        0.21070422714350603,
        0.03571428571428571,
    ]
    barycentric = []
    for left_index in range(8):
        product = 1.0
        for right_index in range(8):
            if right_index != left_index:
                product = product * (points[left_index] - points[right_index])
        barycentric.append(1.0 / product)
    derivative = np.zeros((8, 8))
    for left_index in range(8):
        row_total = 0.0
        for right_index in range(8):
            if left_index != right_index:
                entry = (
                    barycentric[right_index]
                    / barycentric[left_index]
                    / (points[left_index] - points[right_index])
                )
                derivative[left_index, right_index] = entry
                row_total = row_total + entry
        derivative[left_index, left_index] = -row_total
    return (jnp.asarray(derivative, dtype=jnp.float32), jnp.asarray(weights, dtype=jnp.float32))


def gradient(quantity, derivative):
    along_i = jnp.einsum("pi,gijke->gpjke", derivative, quantity, precision=highest)
    along_j = jnp.einsum("pj,gijke->gipke", derivative, quantity, precision=highest)
    along_k = jnp.einsum("pk,gijke->gijpe", derivative, quantity, precision=highest)
    return (along_i, along_j, along_k)


def transposed(quantity, derivative, direction):
    if direction == 0:
        return jnp.einsum("ip,gijke->gpjke", derivative, quantity, precision=highest)
    if direction == 1:
        return jnp.einsum("jp,gijke->gipke", derivative, quantity, precision=highest)
    return jnp.einsum("kp,gijke->gijpe", derivative, quantity, precision=highest)


def forward_terms(quantity, velocity, mass_cube, diffusivity, derivative):
    gradients = gradient(quantity, derivative)
    advect = velocity[0] * gradients[0] + velocity[1] * gradients[1] + velocity[2] * gradients[2]
    diffuse = transposed(mass_cube * gradients[0], derivative, 0)
    diffuse = diffuse + transposed(mass_cube * gradients[1], derivative, 1)
    diffuse = diffuse + transposed(mass_cube * gradients[2], derivative, 2)
    return -(mass_cube * advect) - diffusivity[:, None, None, None, None] * diffuse


def adjoint_terms(quantity, velocity, mass_cube, diffusivity, derivative):
    gradients = gradient(quantity, derivative)
    scaled = diffusivity[:, None, None, None, None]
    summed = transposed(mass_cube * (velocity[0] * quantity + scaled * gradients[0]), derivative, 0)
    summed = summed + transposed(
        mass_cube * (velocity[1] * quantity + scaled * gradients[1]), derivative, 1
    )
    summed = summed + transposed(
        mass_cube * (velocity[2] * quantity + scaled * gradients[2]), derivative, 2
    )
    return -summed


def swap_sides(face_pair):
    return extended(face_pair, (("elem", 0),), 1)


def row_neighbour(face_values, offset):
    return from_behind(face_values, "elem", offset)


def assemble(values, place, slab_row, columns):
    upper_face = values[:, :, :, 7, :]
    lower_face = values[:, :, :, 0, :]
    joined = upper_face[..., :-1] + lower_face[..., 1:]
    new_upper = jnp.concatenate([joined, upper_face[..., -1:]], axis=-1)
    new_lower = jnp.concatenate([lower_face[..., :1], joined], axis=-1)
    values = jnp.concatenate(
        [new_lower[:, :, :, None], values[:, :, :, 1:7], new_upper[:, :, :, None]], axis=3
    )
    below_ok = (place > 0).astype(jnp.float32)
    above_ok = (place < columns - 1).astype(jnp.float32)
    row_low_ok = (slab_row > 0).astype(jnp.float32)
    row_high_ok = (slab_row < DA - 1).astype(jnp.float32)
    padded = swap_sides(jnp.stack([values[:, :, 0], values[:, :, 7]]))
    values = values.at[:, :, 0].add(below_ok * padded[0])
    values = values.at[:, :, 7].add(above_ok * padded[3])
    from_lower = row_neighbour(values[:, 7], columns)
    from_upper = row_neighbour(values[:, 0], -columns)
    values = values.at[:, 0].add(row_low_ok * from_lower)
    values = values.at[:, 7].add(row_high_ok * from_upper)
    return values


def shards(moment_fields, adjoint_fields, velocity, mass_weights, diffusivity, numbering):
    derivative, weights = gll_tables()
    height_count = numbering.shape[0]
    count = moment_fields.shape[0]
    devices_all = lax.axis_size("elem")
    columns = devices_all // DA
    column = (lax.axis_index("elem") + columns // 2) % devices_all
    place = column % columns
    slab_row = column // columns
    height = numbering % height_count
    slot_index = lax.iota(jnp.int32, height_count)
    inverse = jnp.sum(
        jnp.where(height[:, None] == slot_index[None, :], slot_index[:, None], 0), axis=0
    )
    weight_cube = weights[:, None, None] * weights[None, :, None] * weights[None, None, :]
    mass_cube = (
        jnp.take(mass_weights, inverse, axis=-1).reshape(8, 8, 8, height_count)
        * weight_cube[:, :, :, None]
    )
    flow = jnp.take(velocity, inverse, axis=-1).reshape(3, 8, 8, 8, height_count)
    fields_now = jnp.take(moment_fields, inverse, axis=-1).reshape(count, 8, 8, 8, height_count)
    adjoint_now = jnp.take(adjoint_fields, inverse, axis=-1).reshape(count, 8, 8, 8, height_count)
    mass_sum = assemble(mass_cube[None], place, slab_row, columns)[0]
    for step_index in range(2):
        terms = forward_terms(fields_now, flow, mass_cube, diffusivity, derivative)
        fields_now = fields_now + time_step * assemble(terms, place, slab_row, columns) / mass_sum
    for step_index in range(2):
        gathered = assemble(adjoint_now / mass_sum, place, slab_row, columns)
        adjoint_now = adjoint_now + time_step * adjoint_terms(
            gathered, flow, mass_cube, diffusivity, derivative
        )
    moments = jnp.take(fields_now.reshape(count, 512, height_count), height, axis=-1)
    sensitivities = jnp.take(adjoint_now.reshape(count, 512, height_count), height, axis=-1)
    return (moments, sensitivities)


def solution(mesh):
    in_specs = (
        P(None, None, "elem"),
        P(None, None, "elem"),
        P(None, None, "elem"),
        P(None, "elem"),
        P(),
        P("elem"),
    )
    out_specs = (P(None, None, "elem"), P(None, None, "elem"))
    return jax.shard_map(shards, mesh=mesh, in_specs=in_specs, out_specs=out_specs, check_vma=False)
```

profile of v0, /device:TPU:64, one launch (start us, length us, event | category | flops | bytes accessed | tf_op | source)
XLA Modules:
  0.0 192.0 jit_solution(3710935455292315207)
XLA Ops:
  6.6 6.2 %collective-permute-start.5 = (f32[1,1,8,8,128]{4,3,2,1,0:T(8,128)S(1)}, f32[1,1,8,8,128]{4,3,2,1,0:T(8,128)S(1)}, u32[]{:S(2)}, u32[]{:S(2)}) collective-permute-start(f32[1,1,8,8,128]{4,3,2,1,0:T(8,128)S(1)} %get-tuple-element.299), channel_id=1, source_target_pairs={{1,0},{2,1},{3,2},{4,3},{5,4},{6,5},{7,6},{8,7},{9,8},{10,9},{11,1... | collective-permute-start | bytes 98312 | tf_op jit(solution)/shard_map/ppermute | solution.py:23
  15.2 2.4 %gather_fusion.1 = f32[128,3,512]{2,1,0:T(4,128)S(1)} fusion(f32[3,512,128]{1,0,2:T(4,128)} %copy.905, s32[1024]{0:T(1024)S(1)} %pad_clamp_fusion.2), kind=kCustom, calls=%fused_computation.clone | custom fusion | bytes 1573376 | tf_op jit(solution)/shard_map/jit(_take)/gather | solution.py:168
  17.6 2.1 %gather_fusion.2 = f32[128,3,512]{2,1,0:T(4,128)} fusion(f32[3,512,128]{1,0,2:T(4,128)S(1)} %copy.910, s32[1024]{0:T(1024)S(1)} %pad_clamp_fusion.2), kind=kCustom, calls=%fused_computation.1.clone | custom fusion | bytes 1573376 | tf_op jit(solution)/shard_map/jit(_take)/gather | solution.py:167
  20.2 2.1 %gather_fusion.4 = f32[128,3,512]{2,1,0:T(4,128)} fusion(f32[3,512,128]{1,0,2:T(4,128)S(1)} %copy.988, s32[1024]{0:T(1024)S(1)} %pad_clamp_fusion.2), kind=kCustom, calls=%fused_computation.3.clone | custom fusion | bytes 1573376 | tf_op jit(solution)/shard_map/jit(_take)/gather | solution.py:169
  22.3 3.6 %select_bitcast_fusion.1 = (f32[3,512,128]{1,0,2:T(4,128)}, f32[3,512,128]{1,0,2:T(4,128)}, f32[3,512,128]{1,0,2:T(4,128)S(1)}) fusion(f32[128,3,512]{2,1,0:T(4,128)} %gather_fusion.4, pred[128]{0:T(512)(128)(4,1)S(1)} %compare_and_fusion.1, f32[128,3,512]{2,1,0:T(4,128)} %gather_fusion.2, f32[128,3,512]{2,1,0:T(4,128)S(1)} %gather_fusion.1), kind=kLoop, calls=%fused_computation.26 | loop fusion | flops 589824 | bytes 4718720 | tf_op jit(solution)/shard_map/jit(_take)/select_n | solution.py:169
  29.9 2.1 %fusion.62 = f32[3,8,8,128,8]{3,4,2,1,0:T(8,128)} fusion(f32[8,8,1,1,1]{1,0,4,3,2:T(8,128)S(1)} %copy-done.26, f32[3,8,8,8,128]{4,3,0,1,2:T(8,128)S(1)} %bitcast_multiply_fusion.6), kind=kOutput, calls=%fused_computation.112 | convolution fusion | flops 18874368 | bytes 1573120 | tf_op jit(solution)/shard_map/jp,gijke->gipke/dot_general | solution.py:91
  38.5 1.9 fusion.68
  41.1 1.9 %fusion.7 = f32[3,8,8,8,128]{4,3,0,1,2:T(8,128)S(1)} fusion(f32[8,8,1,1,1]{1,0,2,3,4:T(8,128)S(1)} %copy-done.31, f32[3,8,8,128,8]{3,4,2,1,0:T(8,128)S(1)} %copy-done.13, f32[3,8,8,128,8]{3,4,2,1,0:T(8,128)S(1)} %fusion.68, f32[3,8,8,8,128]{4,1,3,2,0:T(8,128)S(1)} %convolution_bitcast_fusion.5, f32[3,8,8,8,128]{4,3,0,1,2:T(8,128)S(1)} %copy-done.14, ...), kind=kOutput, calls=%fused_computation.19 | convolution fusion | flops 21495808 | bytes 5769612 | tf_op jit(solution)/shard_map/kp,gijke->gijpe/dot_general | solution.py:92
  47.4 5.7 %collective-permute-start.6 = (f32[1,8,8,128]{3,2,1,0:T(8,128)S(1)}, f32[1,8,8,128]{3,2,1,0:T(8,128)S(1)}, u32[]{:S(2)}, u32[]{:S(2)}) collective-permute-start(f32[1,8,8,128]{3,2,1,0:T(8,128)S(1)} %slice_bitcast_fusion.12), channel_id=1, source_target_pairs={{192,0},{193,1},{194,2},{195,3},{196,4},{197,5},{198,6},{199,7},{2... | collective-permute-start | bytes 98312 | tf_op jit(solution)/shard_map/ppermute | solution.py:33
  56.1 2.7 %collective-permute-start.7 = (f32[1,8,8,128]{3,2,1,0:T(8,128)}, f32[1,8,8,128]{3,2,1,0:T(8,128)}, u32[]{:S(2)}, u32[]{:S(2)}) collective-permute-start(f32[1,8,8,128]{3,2,1,0:T(8,128)} %get-tuple-element.297), channel_id=1, source_target_pairs={{64,0},{65,1},{66,2},{67,3},{68,4},{69,5},{70,6},{71,7},{72,8},{73... | collective-permute-start | bytes 98312 | tf_op jit(solution)/shard_map/ppermute | solution.py:33
  68.2 4.8 %collective-permute-start.1 = (f32[1,3,8,8,128]{4,3,1,2,0:T(8,128)S(1)}, f32[1,3,8,8,128]{4,3,1,2,0:T(8,128)S(1)}, u32[]{:S(2)}, u32[]{:S(2)}) collective-permute-start(f32[1,3,8,8,128]{4,3,1,2,0:T(8,128)S(1)} %get-tuple-element.288), channel_id=1, source_target_pairs={{1,0},{2,1},{3,2},{4,3},{5,4},{6,5},{7,6},{8,7},{9,8},{10,9},{11,1... | collective-permute-start | bytes 294920 | tf_op jit(solution)/shard_map/ppermute | solution.py:23
  75.9 3.7 %collective-permute-start.2 = (f32[3,8,8,128]{3,2,0,1:T(8,128)}, f32[3,8,8,128]{3,2,0,1:T(8,128)}, u32[]{:S(2)}, u32[]{:S(2)}) collective-permute-start(f32[3,8,8,128]{3,2,0,1:T(8,128)} %get-tuple-element.287), channel_id=1, source_target_pairs={{192,0},{193,1},{194,2},{195,3},{196,4},{197,5},{198,6},{199,7},{2... | collective-permute-start | bytes 294920 | tf_op jit(solution)/shard_map/ppermute | solution.py:33
  79.7 4.8 %scatter-add.89 = f32[3,8,8,8,128]{4,2,3,0,1:T(8,128)S(1)} dynamic-update-slice(f32[3,8,8,8,128]{4,2,3,0,1:T(8,128)S(1)} %copy.997, f32[3,8,1,8,128]{4,2,3,0,1:T(1,128)S(1)} %add.297, s32[]{:T(128)} %constant.499.clone.1, s32[]{:T(128)} %constant.499.clone.1, s32[]{:T(128)} %constant.509.clone.1, s32[]{:T(128)} %constant.499.clone.1, s32[]{:T(128)} %constant.499.clone.1) | dynamic-update-slice | bytes 196612 | tf_op jit(solution)/shard_map/scatter-add | solution.py:140
  84.5 4.2 %collective-permute-start.14 = (f32[3,8,8,128]{3,1,2,0:T(8,128)S(1)}, f32[3,8,8,128]{3,1,2,0:T(8,128)S(1)}, u32[]{:S(2)}, u32[]{:S(2)}) collective-permute-start(f32[3,8,8,128]{3,1,2,0:T(8,128)S(1)} %slice_bitcast_fusion.2), channel_id=1, source_target_pairs={{192,0},{193,1},{194,2},{195,3},{196,4},{197,5},{198,6},{199,7},{2... | collective-permute-start | bytes 294920 | tf_op jit(solution)/shard_map/ppermute | solution.py:33
  94.3 1.9 bitcast_multiply_fusion.2
  100.3 5.2 %collective-permute-done.15 = f32[3,8,8,128]{3,1,2,0:T(8,128)S(1)} collective-permute-done((f32[3,8,8,128]{3,1,2,0:T(8,128)S(1)}, f32[3,8,8,128]{3,1,2,0:T(8,128)S(1)}, u32[]{:S(2)}, u32[]{:S(2)}) %collective-permute-start.15) | collective-permute-done | bytes 98336 | tf_op jit(solution)/shard_map/ppermute | solution.py:33
  105.6 1.9 %scatter-add.91 = f32[3,8,8,8,128]{4,1,2,3,0:T(8,128)S(1)} dynamic-update-slice(f32[3,8,8,8,128]{4,1,2,3,0:T(8,128)S(1)} %copy.999, f32[3,1,8,8,128]{4,1,2,3,0:T(1,128)S(1)} %bitcast.407, s32[]{:T(128)} %constant.499.clone.1, s32[]{:T(128)} %constant.509.clone.1, s32[]{:T(128)} %constant.499.clone.1, s32[]{:T(128)} %constant.499.clone.1, s32[]{:T(128)} %constant.499.clone.1) | dynamic-update-slice | bytes 196612 | tf_op jit(solution)/shard_map/scatter-add | solution.py:144
  114.6 2.2 %fusion.17 = (f32[3,8,8,8,128]{4,1,2,3,0:T(8,128)S(1)}, f32[3,8,8,8,128]{4,1,2,3,0:T(8,128)S(1)}, f32[3,8,8,8,128]{4,1,2,3,0:T(8,128)S(1)}) fusion(f32[3,8,8,128,8]{3,4,2,1,0:T(8,128)S(1)} %fusion.45, f32[3,8,8,8,128]{4,1,2,3,0:T(8,128)S(1)} %scatter-add.91, f32[8,8,8,128]{3,0,1,2:T(8,128)S(1)} %copy-done.8, f32[3]{0:T(128)S(1)} %copy-done.32, ...), kind=kLoop, calls=%fused_computation.45 | loop fusion | flops 2949120 | bytes 8650764 | tf_op jit(solution)/shard_map/mul | solution.py:109
  118.5 7.4 %collective-permute-done.8 = f32[1,3,8,8,128]{4,3,1,2,0:T(8,128)S(1)} collective-permute-done((f32[1,3,8,8,128]{4,3,1,2,0:T(8,128)S(1)}, f32[1,3,8,8,128]{4,3,1,2,0:T(8,128)S(1)}, u32[]{:S(2)}, u32[]{:S(2)}) %collective-permute-start.8) | collective-permute-done | bytes 98336 | tf_op jit(solution)/shard_map/ppermute | solution.py:21
  126.1 2.2 %collective-permute-done.9 = f32[1,3,8,8,128]{4,3,1,2,0:T(8,128)S(1)} collective-permute-done((f32[1,3,8,8,128]{4,3,1,2,0:T(8,128)S(1)}, f32[1,3,8,8,128]{4,3,1,2,0:T(8,128)S(1)}, u32[]{:S(2)}, u32[]{:S(2)}) %collective-permute-start.9) | collective-permute-done | bytes 98336 | tf_op jit(solution)/shard_map/ppermute | solution.py:23
  130.2 4.5 %collective-permute-done.10 = f32[3,8,8,128]{3,2,0,1:T(8,128)S(1)} collective-permute-done((f32[3,8,8,128]{3,2,0,1:T(8,128)S(1)}, f32[3,8,8,128]{3,2,0,1:T(8,128)S(1)}, u32[]{:S(2)}, u32[]{:S(2)}) %collective-permute-start.10) | collective-permute-done | bytes 98336 | tf_op jit(solution)/shard_map/ppermute | solution.py:33
  134.7 2.1 %collective-permute-start.11 = (f32[3,8,8,128]{3,2,0,1:T(8,128)S(1)}, f32[3,8,8,128]{3,2,0,1:T(8,128)}, u32[]{:S(2)}, u32[]{:S(2)}) collective-permute-start(f32[3,8,8,128]{3,2,0,1:T(8,128)S(1)} %get-tuple-element.310), channel_id=1, source_target_pairs={{64,0},{65,1},{66,2},{67,3},{68,4},{69,5},{70,6},{71,7},{72,8},{73... | collective-permute-start | bytes 294920 | tf_op jit(solution)/shard_map/ppermute | solution.py:33
  138.4 1.9 %scatter-add.84 = f32[3,8,8,8,128]{4,1,2,3,0:T(8,128)S(1)} dynamic-update-slice(f32[3,8,8,8,128]{4,1,2,3,0:T(8,128)S(1)} %copy_dynamic-update-slice_fusion.2, f32[3,1,8,8,128]{4,1,2,3,0:T(1,128)S(1)} %copy.982, s32[]{:T(128)} %constant.499.clone.1, s32[]{:T(128)} %constant.499.clone.1, s32[]{:T(128)} %constant.499.clone.1, s32[]{:T(128)} %constant.499.clone.1, s32[]{:T(128)} %constant.499.clone.1) | dynamic-update-slice | bytes 196612 | tf_op jit(solution)/shard_map/scatter-add | solution.py:143
  142.9 1.9 %scatter-add.85 = f32[3,8,8,8,128]{4,1,2,3,0:T(8,128)S(1)} dynamic-update-slice(f32[3,8,8,8,128]{4,1,2,3,0:T(8,128)S(1)} %scatter-add.84, f32[3,1,8,8,128]{4,1,2,3,0:T(1,128)S(1)} %copy.984, s32[]{:T(128)} %constant.499.clone.1, s32[]{:T(128)} %constant.509.clone.1, s32[]{:T(128)} %constant.499.clone.1, s32[]{:T(128)} %constant.499.clone.1, s32[]{:T(128)} %constant.499.clone.1) | dynamic-update-slice | bytes 196612 | tf_op jit(solution)/shard_map/scatter-add | solution.py:144
  146.7 8.2 %collective-permute-done.16 = f32[1,3,8,8,128]{4,3,1,2,0:T(8,128)S(1)} collective-permute-done((f32[1,3,8,8,128]{4,3,1,2,0:T(8,128)S(1)}, f32[1,3,8,8,128]{4,3,1,2,0:T(8,128)S(1)}, u32[]{:S(2)}, u32[]{:S(2)}) %collective-permute-start.16) | collective-permute-done | bytes 98336 | tf_op jit(solution)/shard_map/ppermute | solution.py:21
  155.1 2.2 %collective-permute-done.17 = f32[1,3,8,8,128]{4,3,1,2,0:T(8,128)S(1)} collective-permute-done((f32[1,3,8,8,128]{4,3,1,2,0:T(8,128)S(1)}, f32[1,3,8,8,128]{4,3,1,2,0:T(8,128)S(1)}, u32[]{:S(2)}, u32[]{:S(2)}) %collective-permute-start.17) | collective-permute-done | bytes 98336 | tf_op jit(solution)/shard_map/ppermute | solution.py:23
  158.1 2.6 %collective-permute-start.18 = (f32[3,8,8,128]{3,1,2,0:T(8,128)}, f32[3,8,8,128]{3,1,2,0:T(8,128)}, u32[]{:S(2)}, u32[]{:S(2)}) collective-permute-start(f32[3,8,8,128]{3,1,2,0:T(8,128)} %bitcast.110), channel_id=1, source_target_pairs={{192,0},{193,1},{194,2},{195,3},{196,4},{197,5},{198,6},{199,7},{2... | collective-permute-start | bytes 294920 | tf_op jit(solution)/shard_map/ppermute | solution.py:33
  163.1 2.5 %gather_fusion.3 = f32[128,3,512]{2,1,0:T(4,128)S(1)} fusion(f32[3,512,128]{1,0,2:T(4,128)} %copy.987, s32[1024]{0:T(1024)} %pad_clamp_fusion), kind=kCustom, calls=%fused_computation.2.clone | custom fusion | bytes 1573376 | tf_op jit(solution)/shard_map/jit(_take)/gather | solution.py:179
  167.2 1.9 %scatter-add.96 = f32[3,8,8,8,128]{4,1,2,3,0:T(8,128)S(1)} dynamic-update-slice(f32[3,8,8,8,128]{4,1,2,3,0:T(8,128)S(1)} %copy_dynamic-update-slice_fusion, f32[3,1,8,8,128]{4,1,2,3,0:T(1,128)S(1)} %bitcast.408, s32[]{:T(128)} %constant.499.clone.1, s32[]{:T(128)} %constant.499.clone.1, s32[]{:T(128)} %constant.499.clone.1, s32[]{:T(128)} %constant.499.clone.1, s32[]{:T(128)} %constant.499.clone.1) | dynamic-update-slice | bytes 196612 | tf_op jit(solution)/shard_map/scatter-add | solution.py:143
  169.2 4.6 %collective-permute-done.19 = f32[3,8,8,128]{3,1,2,0:T(8,128)S(1)} collective-permute-done((f32[3,8,8,128]{3,1,2,0:T(8,128)S(1)}, f32[3,8,8,128]{3,1,2,0:T(8,128)S(1)}, u32[]{:S(2)}, u32[]{:S(2)}) %collective-permute-start.19) | collective-permute-done | bytes 98336 | tf_op jit(solution)/shard_map/ppermute | solution.py:33
  173.9 1.9 %scatter-add.99 = f32[3,8,8,8,128]{4,1,2,3,0:T(8,128)S(1)} dynamic-update-slice(f32[3,8,8,8,128]{4,1,2,3,0:T(8,128)S(1)} %scatter-add.96, f32[3,1,8,8,128]{4,1,2,3,0:T(1,128)S(1)} %slice_add_fusion, s32[]{:T(128)} %constant.499.clone.1, s32[]{:T(128)} %constant.509.clone.1, s32[]{:T(128)} %constant.499.clone.1, s32[]{:T(128)} %constant.499.clone.1, s32[]{:T(128)} %constant.499.clone.1) | dynamic-update-slice | bytes 196612 | tf_op jit(solution)/shard_map/scatter-add | solution.py:144
  184.4 2.2 %gather_fusion.5 = f32[128,3,512]{2,1,0:T(4,128)} fusion(f32[3,512,128]{1,0,2:T(4,128)S(1)} %copy.1055, s32[1024]{0:T(1024)} %pad_clamp_fusion), kind=kCustom, calls=%fused_computation.4.clone | custom fusion | bytes 1573376 | tf_op jit(solution)/shard_map/jit(_take)/gather | solution.py:180
  (249 shorter events, 84.1 us)
Async XLA Ops:
  4.9 8.4 %copy-start.27 = (f32[3,512,128]{2,1,0:T(8,128)S(1)}, f32[3,512,128]{2,1,0:T(8,128)}, u32[]{:S(2)}) copy-start(f32[3,512,128]{2,1,0:T(8,128)} %param.50) | copy-start | bytes 2359300
  6.6 37.3 %collective-permute-start.4 = (f32[1,1,8,8,128]{4,3,2,1,0:T(8,128)}, f32[1,1,8,8,128]{4,3,2,1,0:T(8,128)}, u32[]{:S(2)}, u32[]{:S(2)}) collective-permute-start(f32[1,1,8,8,128]{4,3,2,1,0:T(8,128)} %get-tuple-element.301), channel_id=1, source_target_pairs={{0,1},{1,2},{2,3},{3,4},{4,5},{5,6},{6,7},{7,8},{8,9},{9,10},{10,1... | collective-permute-start | bytes 98312 | tf_op jit(solution)/shard_map/ppermute | solution.py:21
  6.6 38.7 %collective-permute-start.5 = (f32[1,1,8,8,128]{4,3,2,1,0:T(8,128)S(1)}, f32[1,1,8,8,128]{4,3,2,1,0:T(8,128)S(1)}, u32[]{:S(2)}, u32[]{:S(2)}) collective-permute-start(f32[1,1,8,8,128]{4,3,2,1,0:T(8,128)S(1)} %get-tuple-element.299), channel_id=1, source_target_pairs={{1,0},{2,1},{3,2},{4,3},{5,4},{6,5},{7,6},{8,7},{9,8},{10,9},{11,1... | collective-permute-start | bytes 98312 | tf_op jit(solution)/shard_map/ppermute | solution.py:23
  17.6 2.1 %copy-start.29 = (f32[3,512,128]{2,1,0:T(8,128)S(1)}, f32[3,512,128]{2,1,0:T(8,128)}, u32[]{:S(2)}) copy-start(f32[3,512,128]{2,1,0:T(8,128)} %param.51) | copy-start | bytes 2359300
  29.8 2.1 %copy-start.10 = (f32[3,512,128]{1,0,2:T(4,128)S(1)}, f32[3,512,128]{1,0,2:T(4,128)}, u32[]{:S(2)}) copy-start(f32[3,512,128]{1,0,2:T(4,128)} %get-tuple-element.323) | copy-start | bytes 2359300
  34.0 6.4 %copy-start.4 = (f32[1,512,128]{2,1,0:T(8,128)}, f32[1,512,128]{2,1,0:T(8,128)S(1)}, u32[]{:S(2)}) copy-start(f32[1,512,128]{2,1,0:T(8,128)S(1)} %copy.911) | copy-start | bytes 786436
  38.5 1.9 %copy-start.13 = (f32[3,8,8,128,8]{3,4,2,1,0:T(8,128)S(1)}, f32[3,8,8,128,8]{3,4,2,1,0:T(8,128)}, u32[]{:S(2)}) copy-start(f32[3,8,8,128,8]{3,4,2,1,0:T(8,128)} %fusion.62) | copy-start | bytes 2359300
  38.5 1.9 %copy-start.14 = (f32[3,8,8,8,128]{4,3,0,1,2:T(8,128)S(1)}, f32[3,8,8,8,128]{4,3,0,1,2:T(8,128)}, u32[]{:S(2)}) copy-start(f32[3,8,8,8,128]{4,3,0,1,2:T(8,128)} %convolution_bitcast_fusion.4) | copy-start | bytes 2359300
  38.5 2.0 %copy-start.21 = (f32[1,512,128]{2,1,0:T(8,128)S(1)}, f32[1,512,128]{2,1,0:T(8,128)}, u32[]{:S(2)}) copy-start(f32[1,512,128]{2,1,0:T(8,128)} %copy.920) | copy-start | bytes 786436
  47.4 7.3 %collective-permute-start.6 = (f32[1,8,8,128]{3,2,1,0:T(8,128)S(1)}, f32[1,8,8,128]{3,2,1,0:T(8,128)S(1)}, u32[]{:S(2)}, u32[]{:S(2)}) collective-permute-start(f32[1,8,8,128]{3,2,1,0:T(8,128)S(1)} %slice_bitcast_fusion.12), channel_id=1, source_target_pairs={{192,0},{193,1},{194,2},{195,3},{196,4},{197,5},{198,6},{199,7},{2... | collective-permute-start | bytes 98312 | tf_op jit(solution)/shard_map/ppermute | solution.py:33
  56.1 7.1 %collective-permute-start.7 = (f32[1,8,8,128]{3,2,1,0:T(8,128)}, f32[1,8,8,128]{3,2,1,0:T(8,128)}, u32[]{:S(2)}, u32[]{:S(2)}) collective-permute-start(f32[1,8,8,128]{3,2,1,0:T(8,128)} %get-tuple-element.297), channel_id=1, source_target_pairs={{64,0},{65,1},{66,2},{67,3},{68,4},{69,5},{70,6},{71,7},{72,8},{73... | collective-permute-start | bytes 98312 | tf_op jit(solution)/shard_map/ppermute | solution.py:33
  58.8 8.4 %collective-permute-start = (f32[1,3,8,8,128]{4,3,1,2,0:T(8,128)S(1)}, f32[1,3,8,8,128]{4,3,1,2,0:T(8,128)}, u32[]{:S(2)}, u32[]{:S(2)}) collective-permute-start(f32[1,3,8,8,128]{4,3,1,2,0:T(8,128)S(1)} %slice_bitcast_fusion.7), channel_id=1, source_target_pairs={{0,1},{1,2},{2,3},{3,4},{4,5},{5,6},{6,7},{7,8},{8,9},{9,10},{10,1... | collective-permute-start | bytes 294920 | tf_op jit(solution)/shard_map/ppermute | solution.py:21
  66.0 8.3 %collective-permute-start.12 = (f32[1,3,8,8,128]{4,3,1,2,0:T(8,128)S(1)}, f32[1,3,8,8,128]{4,3,1,2,0:T(8,128)S(1)}, u32[]{:S(2)}, u32[]{:S(2)}) collective-permute-start(f32[1,3,8,8,128]{4,3,1,2,0:T(8,128)S(1)} %slice_bitcast_fusion.3), channel_id=1, source_target_pairs={{0,1},{1,2},{2,3},{3,4},{4,5},{5,6},{6,7},{7,8},{8,9},{9,10},{10,1... | collective-permute-start | bytes 294920 | tf_op jit(solution)/shard_map/ppermute | solution.py:21
  68.2 7.0 %collective-permute-start.1 = (f32[1,3,8,8,128]{4,3,1,2,0:T(8,128)S(1)}, f32[1,3,8,8,128]{4,3,1,2,0:T(8,128)S(1)}, u32[]{:S(2)}, u32[]{:S(2)}) collective-permute-start(f32[1,3,8,8,128]{4,3,1,2,0:T(8,128)S(1)} %get-tuple-element.288), channel_id=1, source_target_pairs={{1,0},{2,1},{3,2},{4,3},{5,4},{6,5},{7,6},{8,7},{9,8},{10,9},{11,1... | collective-permute-start | bytes 294920 | tf_op jit(solution)/shard_map/ppermute | solution.py:23
  74.7 4.8 %collective-permute-start.13 = (f32[1,3,8,8,128]{4,3,1,2,0:T(8,128)S(1)}, f32[1,3,8,8,128]{4,3,1,2,0:T(8,128)S(1)}, u32[]{:S(2)}, u32[]{:S(2)}) collective-permute-start(f32[1,3,8,8,128]{4,3,1,2,0:T(8,128)S(1)} %get-tuple-element.273), channel_id=1, source_target_pairs={{1,0},{2,1},{3,2},{4,3},{5,4},{6,5},{7,6},{8,7},{9,8},{10,9},{11,1... | collective-permute-start | bytes 294920 | tf_op jit(solution)/shard_map/ppermute | solution.py:23
  75.9 12.9 %collective-permute-start.2 = (f32[3,8,8,128]{3,2,0,1:T(8,128)}, f32[3,8,8,128]{3,2,0,1:T(8,128)}, u32[]{:S(2)}, u32[]{:S(2)}) collective-permute-start(f32[3,8,8,128]{3,2,0,1:T(8,128)} %get-tuple-element.287), channel_id=1, source_target_pairs={{192,0},{193,1},{194,2},{195,3},{196,4},{197,5},{198,6},{199,7},{2... | collective-permute-start | bytes 294920 | tf_op jit(solution)/shard_map/ppermute | solution.py:33
  79.6 10.1 %collective-permute-start.3 = (f32[3,8,8,128]{3,2,0,1:T(8,128)}, f32[3,8,8,128]{3,2,0,1:T(8,128)}, u32[]{:S(2)}, u32[]{:S(2)}) collective-permute-start(f32[3,8,8,128]{3,2,0,1:T(8,128)} %get-tuple-element.285), channel_id=1, source_target_pairs={{64,0},{65,1},{66,2},{67,3},{68,4},{69,5},{70,6},{71,7},{72,8},{73... | collective-permute-start | bytes 294920 | tf_op jit(solution)/shard_map/ppermute | solution.py:33
  84.5 6.2 %copy-start.2 = (f32[3,8,8,8,128]{4,2,3,0,1:T(8,128)}, f32[3,8,8,8,128]{4,2,3,0,1:T(8,128)S(1)}, u32[]{:S(2)}) copy-start(f32[3,8,8,8,128]{4,2,3,0,1:T(8,128)S(1)} %scatter-add.89) | copy-start | bytes 2359300
  84.5 4.2 %copy-start.30 = (f32[3,1,8,8,128]{4,3,0,1,2:T(8,128)S(1)}, f32[3,1,8,8,128]{4,3,0,1,2:T(8,128)}, u32[]{:S(2)}) copy-start(f32[3,1,8,8,128]{4,3,0,1,2:T(8,128)} %get-tuple-element.286) | copy-start | bytes 294916
  84.5 13.3 %collective-permute-start.14 = (f32[3,8,8,128]{3,1,2,0:T(8,128)S(1)}, f32[3,8,8,128]{3,1,2,0:T(8,128)S(1)}, u32[]{:S(2)}, u32[]{:S(2)}) collective-permute-start(f32[3,8,8,128]{3,1,2,0:T(8,128)S(1)} %slice_bitcast_fusion.2), channel_id=1, source_target_pairs={{192,0},{193,1},{194,2},{195,3},{196,4},{197,5},{198,6},{199,7},{2... | collective-permute-start | bytes 294920 | tf_op jit(solution)/shard_map/ppermute | solution.py:33
  94.3 1.9 copy-start
  96.2 1.7 copy-start.3
  97.9 7.7 %collective-permute-start.15 = (f32[3,8,8,128]{3,1,2,0:T(8,128)S(1)}, f32[3,8,8,128]{3,1,2,0:T(8,128)S(1)}, u32[]{:S(2)}, u32[]{:S(2)}) collective-permute-start(f32[3,8,8,128]{3,1,2,0:T(8,128)S(1)} %get-tuple-element.271), channel_id=1, source_target_pairs={{64,0},{65,1},{66,2},{67,3},{68,4},{69,5},{70,6},{71,7},{72,8},{73... | collective-permute-start | bytes 294920 | tf_op jit(solution)/shard_map/ppermute | solution.py:33
  117.3 8.6 %collective-permute-start.8 = (f32[1,3,8,8,128]{4,3,1,2,0:T(8,128)S(1)}, f32[1,3,8,8,128]{4,3,1,2,0:T(8,128)S(1)}, u32[]{:S(2)}, u32[]{:S(2)}) collective-permute-start(f32[1,3,8,8,128]{4,3,1,2,0:T(8,128)S(1)} %bitcast.420), channel_id=1, source_target_pairs={{0,1},{1,2},{2,3},{3,4},{4,5},{5,6},{6,7},{7,8},{8,9},{9,10},{10,1... | collective-permute-start | bytes 294920 | tf_op jit(solution)/shard_map/ppermute | solution.py:21
  125.9 2.3 %collective-permute-start.9 = (f32[1,3,8,8,128]{4,3,1,2,0:T(8,128)S(1)}, f32[1,3,8,8,128]{4,3,1,2,0:T(8,128)S(1)}, u32[]{:S(2)}, u32[]{:S(2)}) collective-permute-start(f32[1,3,8,8,128]{4,3,1,2,0:T(8,128)S(1)} %get-tuple-element.312), channel_id=1, source_target_pairs={{1,0},{2,1},{3,2},{4,3},{5,4},{6,5},{7,6},{8,7},{9,8},{10,9},{11,1... | collective-permute-start | bytes 294920 | tf_op jit(solution)/shard_map/ppermute | solution.py:23
  128.4 6.2 %collective-permute-start.10 = (f32[3,8,8,128]{3,2,0,1:T(8,128)S(1)}, f32[3,8,8,128]{3,2,0,1:T(8,128)S(1)}, u32[]{:S(2)}, u32[]{:S(2)}) collective-permute-start(f32[3,8,8,128]{3,2,0,1:T(8,128)S(1)} %bitcast.419), channel_id=1, source_target_pairs={{192,0},{193,1},{194,2},{195,3},{196,4},{197,5},{198,6},{199,7},{2... | collective-permute-start | bytes 294920 | tf_op jit(solution)/shard_map/ppermute | solution.py:33
  134.7 7.1 %collective-permute-start.11 = (f32[3,8,8,128]{3,2,0,1:T(8,128)S(1)}, f32[3,8,8,128]{3,2,0,1:T(8,128)}, u32[]{:S(2)}, u32[]{:S(2)}) collective-permute-start(f32[3,8,8,128]{3,2,0,1:T(8,128)S(1)} %get-tuple-element.310), channel_id=1, source_target_pairs={{64,0},{65,1},{66,2},{67,3},{68,4},{69,5},{70,6},{71,7},{72,8},{73... | collective-permute-start | bytes 294920 | tf_op jit(solution)/shard_map/ppermute | solution.py:33
  146.6 8.3 %collective-permute-start.16 = (f32[1,3,8,8,128]{4,3,1,2,0:T(8,128)S(1)}, f32[1,3,8,8,128]{4,3,1,2,0:T(8,128)S(1)}, u32[]{:S(2)}, u32[]{:S(2)}) collective-permute-start(f32[1,3,8,8,128]{4,3,1,2,0:T(8,128)S(1)} %bitcast.421), channel_id=1, source_target_pairs={{0,1},{1,2},{2,3},{3,4},{4,5},{5,6},{6,7},{7,8},{8,9},{9,10},{10,1... | collective-permute-start | bytes 294920 | tf_op jit(solution)/shard_map/ppermute | solution.py:21
  154.9 2.3 %collective-permute-start.17 = (f32[1,3,8,8,128]{4,3,1,2,0:T(8,128)S(1)}, f32[1,3,8,8,128]{4,3,1,2,0:T(8,128)S(1)}, u32[]{:S(2)}, u32[]{:S(2)}) collective-permute-start(f32[1,3,8,8,128]{4,3,1,2,0:T(8,128)S(1)} %get-tuple-element.304), channel_id=1, source_target_pairs={{1,0},{2,1},{3,2},{4,3},{5,4},{6,5},{7,6},{8,7},{9,8},{10,9},{11,1... | collective-permute-start | bytes 294920 | tf_op jit(solution)/shard_map/ppermute | solution.py:23
  158.1 2.6 %copy-start.34 = (s32[128]{0:T(128)S(1)}, s32[128]{0:T(128)}, u32[]{:S(2)}) copy-start(s32[128]{0:T(128)} %get-tuple-element.325) | copy-start | bytes 1540
  158.1 8.3 %collective-permute-start.18 = (f32[3,8,8,128]{3,1,2,0:T(8,128)}, f32[3,8,8,128]{3,1,2,0:T(8,128)}, u32[]{:S(2)}, u32[]{:S(2)}) collective-permute-start(f32[3,8,8,128]{3,1,2,0:T(8,128)} %bitcast.110), channel_id=1, source_target_pairs={{192,0},{193,1},{194,2},{195,3},{196,4},{197,5},{198,6},{199,7},{2... | collective-permute-start | bytes 294920 | tf_op jit(solution)/shard_map/ppermute | solution.py:33
  165.6 8.2 %collective-permute-start.19 = (f32[3,8,8,128]{3,1,2,0:T(8,128)S(1)}, f32[3,8,8,128]{3,1,2,0:T(8,128)S(1)}, u32[]{:S(2)}, u32[]{:S(2)}) collective-permute-start(f32[3,8,8,128]{3,1,2,0:T(8,128)S(1)} %bitcast.411), channel_id=1, source_target_pairs={{64,0},{65,1},{66,2},{67,3},{68,4},{69,5},{70,6},{71,7},{72,8},{73... | collective-permute-start | bytes 294920 | tf_op jit(solution)/shard_map/ppermute | solution.py:33
  (24 other events, 25.7 us)
where the time goes:
time: 196 us; the launch traced here: 192 us
  local copies, waits for them, and re-layouts  57 us (29%)
  waiting for transfers between devices  39.9 us (20%)
  starting transfers between devices  34.4 us (18%)
  matrix products  29.2 us (15%)
  other arithmetic  29.1 us (15%)
  between operations  2.38 us (1%)
    ppermute x10, starting transfers between devices, from_behind(): return lax.ppermute(block, axis, route)  22.8 us
    ppermute x5, waiting for transfers between devices, extended(): lax.ppermute(tail, axis, [(i, (i + 1) % count) for i in range(count)])  18.2 us
    ppermute x10, waiting for transfers between devices, from_behind(): return lax.ppermute(block, axis, route)  17.1 us
    unnamed x83, local copies, waits for them, and re-layouts  12.5 us
    ppermute x5, starting transfers between devices, extended(): lax.ppermute(head, axis, [((i + 1) % count, i) for i in range(count)])  11.2 us
    scatter-add x4, local copies, waits for them, and re-layouts, assemble(): values = values.at[:, 7].add(row_high_ok * from_upper)  6.66 us
    dot_general x4, matrix products, transposed(): jnp.einsum('kp,gijke->gijpe', derivative, quantity, precision=highest)  5.98 us
    dot_general x4, matrix products, transposed(): jnp.einsum('jp,gijke->gipke', derivative, quantity, precision=highest)  5.59 us
  transfers between devices with their start and end apart: 20, of which 12 were waited for; matrix products, arithmetic and copies ran while one was open for 36% of the time, Pallas kernels for 0%

commit v1 on v0

v1 whole, which is shorter than its diff:
```python
import functools

import jax
import jax.numpy as jnp
import numpy as np
from jax import lax
from jax.experimental import pallas as pl
from jax.experimental.pallas import tpu as pltpu
from jax.sharding import PartitionSpec as P

DA = 4

time_step = 0.001


def gll_tables():
    points = [
        -1.0,
        -0.8717401485096066,
        -0.5917001814331423,
        -0.2092992179024789,
        0.2092992179024789,
        0.5917001814331423,
        0.8717401485096066,
        1.0,
    ]
    weights = [
        0.03571428571428571,
        0.21070422714350603,
        0.3411226924835044,
        0.4124587946587038,
        0.4124587946587038,
        0.3411226924835044,
        0.21070422714350603,
        0.03571428571428571,
    ]
    barycentric = []
    for left_index in range(8):
        product = 1.0
        for right_index in range(8):
            if right_index != left_index:
                product = product * (points[left_index] - points[right_index])
        barycentric.append(1.0 / product)
    derivative = np.zeros((8, 8))
    for left_index in range(8):
        row_total = 0.0
        for right_index in range(8):
            if left_index != right_index:
                entry = (
                    barycentric[right_index]
                    / barycentric[left_index]
                    / (points[left_index] - points[right_index])
                )
                derivative[left_index, right_index] = entry
                row_total = row_total + entry
        derivative[left_index, left_index] = -row_total
    return derivative.astype(np.float32), np.asarray(weights, dtype=np.float32)


DM, WEIGHTS = gll_tables()
DMC = [[float(DM[p, q]) for q in range(8)] for p in range(8)]


def shift_tables():
    fwd = np.zeros((8, 8, 128), np.float32)
    bwd = np.zeros((8, 8, 128), np.float32)
    for s in range(8):
        for p in range(8):
            fwd[s, p, :] = DM[p, (p - s) % 8]
            bwd[s, p, :] = DM[(p - s) % 8, p]
    return np.concatenate([fwd, bwd], axis=0)


def along_major(v, axis, transpose):
    parts = []
    for p in range(8):
        acc = None
        for q in range(8):
            c = DMC[q][p] if transpose else DMC[p][q]
            term = c * (v[q] if axis == 0 else v[:, q])
            acc = term if acc is None else acc + term
        parts.append(acc)
    return jnp.stack(parts, axis=axis)


def along_sublane(v, tab_ref, base):
    acc = None
    for s in range(8):
        rolled = v if s == 0 else pltpu.roll(v, s, 2)
        term = tab_ref[base + s] * rolled
        acc = term if acc is None else acc + term
    return acc


def gradients(v, tab_ref):
    return (
        along_major(v, 0, False),
        along_major(v, 1, False),
        along_sublane(v, tab_ref, 0),
    )


def transposed(v, tab_ref, direction):
    if direction == 0:
        return along_major(v, 0, True)
    if direction == 1:
        return along_major(v, 1, True)
    return along_sublane(v, tab_ref, 8)


def forward_terms(q, flow, mass, kappa, tab_ref):
    g = gradients(q, tab_ref)
    advect = flow[0] * g[0] + flow[1] * g[1] + flow[2] * g[2]
    diffuse = transposed(mass * g[0], tab_ref, 0)
    diffuse = diffuse + transposed(mass * g[1], tab_ref, 1)
    diffuse = diffuse + transposed(mass * g[2], tab_ref, 2)
    return -(mass * advect) - kappa * diffuse


def adjoint_terms(q, flow, mass, kappa, tab_ref):
    g = gradients(q, tab_ref)
    summed = transposed(mass * (flow[0] * q + kappa * g[0]), tab_ref, 0)
    summed = summed + transposed(mass * (flow[1] * q + kappa * g[1]), tab_ref, 1)
    summed = summed + transposed(mass * (flow[2] * q + kappa * g[2]), tab_ref, 2)
    return -summed


def z_assemble(v):
    shape = v.shape
    sub = lax.broadcasted_iota(jnp.int32, shape, 2)
    lane = lax.broadcasted_iota(jnp.int32, shape, 3)
    below = pltpu.roll(pltpu.roll(v, 1, 2), 1, 3)
    above = pltpu.roll(pltpu.roll(v, 7, 2), 127, 3)
    zero = jnp.zeros_like(v)
    v = v + jnp.where((sub == 0) & (lane > 0), below, zero)
    return v + jnp.where((sub == 7) & (lane < 127), above, zero)


def kernel(
    ndev,
    cols,
    fld_ref,
    adj_ref,
    vel_ref,
    mass_ref,
    tab_ref,
    kap_ref,
    out_f_ref,
    out_a_ref,
    x1,
    x2,
    x3,
    ms_ref,
    f1_ref,
    a1_ref,
    sj1,
    rj1,
    si1,
    ri1,
    sj2,
    rj2,
    si2,
    ri2,
    sj3,
    rj3,
    si3,
    ri3,
    ssem,
    rsem,
):
    me = lax.axis_index("elem")
    column = (me + cols // 2) % ndev
    place = column % cols
    row = column // cols
    right = (me + 1) % ndev
    left = (me + ndev - 1) % ndev
    up = (me + cols) % ndev
    down = (me + ndev - cols) % ndev
    has_right = place < cols - 1
    has_left = place > 0
    has_up = row < DA - 1
    has_down = row > 0

    barrier = pltpu.get_barrier_semaphore()
    for nb in (left, right, up, down):
        pl.semaphore_signal(barrier, inc=1, device_id=(nb,), device_id_type=pl.DeviceIdType.MESH)
    pl.semaphore_wait(barrier, 4)

    def exchange(x, nf, rnd, sj, rj, si, ri):
        for f in range(nf):
            x[f] = z_assemble(x[f])
        for f in range(nf):
            sj[0, f] = x[f, :, 0]
            sj[1, f] = x[f, :, 7]

        def pair(s_buf, r_buf, d, hi, lo, has_hi, has_lo, fixup):
            c_hi = pltpu.make_async_remote_copy(
                s_buf.at[1], r_buf.at[0], ssem.at[rnd, d, 1], rsem.at[rnd, d, 0],
                device_id=(hi,), device_id_type=pl.DeviceIdType.MESH,
            )
            c_lo = pltpu.make_async_remote_copy(
                s_buf.at[0], r_buf.at[1], ssem.at[rnd, d, 0], rsem.at[rnd, d, 1],
                device_id=(lo,), device_id_type=pl.DeviceIdType.MESH,
            )

            @pl.when(has_hi)
            def _():
                c_hi.start()

            @pl.when(has_lo)
            def _():
                c_lo.start()

            @pl.when(has_hi)
            def _():
                c_hi.wait_send()
                c_lo.wait_recv()
                fixup(7, r_buf.at[1])

            @pl.when(has_lo)
            def _():
                c_lo.wait_send()
                c_hi.wait_recv()
                fixup(0, r_buf.at[0])

        def fix_j(side, buf):
            for f in range(nf):
                x[f, :, side] = x[f, :, side] + buf[f]

        pair(sj, rj, 0, right, left, has_right, has_left, fix_j)

        for f in range(nf):
            si[0, f] = x[f, 0]
            si[1, f] = x[f, 7]

        def fix_i(side, buf):
            for f in range(nf):
                x[f, side] = x[f, side] + buf[f]

        pair(si, ri, 1, up, down, has_up, has_down, fix_i)

    def flow():
        return (vel_ref[0], vel_ref[1], vel_ref[2])

    x1[0] = mass_ref[...]

    def r1_body(f, c):
        x1[f + 1] = forward_terms(fld_ref[f], flow(), mass_ref[...], kap_ref[f], tab_ref)
        return c

    lax.fori_loop(0, 3, r1_body, 0)
    exchange(x1, 4, 0, sj1, rj1, si1, ri1)
    ms_ref[...] = x1[0]

    def f1_body(f, c):
        f1_ref[f] = fld_ref[f] + time_step * x1[f + 1] / ms_ref[...]
        x2[f + 3] = adj_ref[f] / ms_ref[...]
        return c

    lax.fori_loop(0, 3, f1_body, 0)

    def r2_body(f, c):
        x2[f] = forward_terms(f1_ref[f], flow(), mass_ref[...], kap_ref[f], tab_ref)
        return c

    lax.fori_loop(0, 3, r2_body, 0)
    exchange(x2, 6, 1, sj2, rj2, si2, ri2)

    def a1_body(f, c):
        out_f_ref[f] = f1_ref[f] + time_step * x2[f] / ms_ref[...]
        a1 = adj_ref[f] + time_step * adjoint_terms(x2[f + 3], flow(), mass_ref[...], kap_ref[f], tab_ref)
        a1_ref[f] = a1
        x3[f] = a1 / ms_ref[...]
        return c

    lax.fori_loop(0, 3, a1_body, 0)

    exchange(x3, 3, 2, sj3, rj3, si3, ri3)

    def a2_body(f, c):
        out_a_ref[f] = a1_ref[f] + time_step * adjoint_terms(x3[f], flow(), mass_ref[...], kap_ref[f], tab_ref)
        return c

    lax.fori_loop(0, 3, a2_body, 0)


def fused(fields, adjoint, flow, mass, table, kappa, ndev, cols):
    cube = (8, 8, 8, 128)
    f32 = jnp.float32
    vmem = pl.BlockSpec(memory_space=pltpu.VMEM)
    smem = pl.BlockSpec(memory_space=pltpu.SMEM)
    scratch = [
        pltpu.VMEM((4,) + cube, f32),
        pltpu.VMEM((6,) + cube, f32),
        pltpu.VMEM((3,) + cube, f32),
        pltpu.VMEM(cube, f32),
        pltpu.VMEM((3,) + cube, f32),
        pltpu.VMEM((3,) + cube, f32),
    ]
    for nf in (4, 6, 3):
        for _ in range(4):
            scratch.append(pltpu.VMEM((2, nf, 8, 8, 128), f32))
    scratch += [pltpu.SemaphoreType.DMA((3, 2, 2)), pltpu.SemaphoreType.DMA((3, 2, 2))]
    return pl.pallas_call(
        functools.partial(kernel, ndev, cols),
        out_shape=(jax.ShapeDtypeStruct((3,) + cube, f32), jax.ShapeDtypeStruct((3,) + cube, f32)),
        in_specs=[vmem, vmem, vmem, vmem, vmem, smem],
        out_specs=(vmem, vmem),
        scratch_shapes=scratch,
        compiler_params=pltpu.CompilerParams(
            collective_id=0, has_side_effects=True, vmem_limit_bytes=60 * 1024 * 1024
        ),
    )(fields, adjoint, flow, mass, table, kappa)


def shards(moment_fields, adjoint_fields, velocity, mass_weights, diffusivity, numbering):
    height_count = numbering.shape[0]
    count = moment_fields.shape[0]
    ndev = lax.axis_size("elem")
    cols = ndev // DA
    height = numbering % height_count
    slot_index = lax.iota(jnp.int32, height_count)
    inverse = jnp.sum(
        jnp.where(height[:, None] == slot_index[None, :], slot_index[:, None], 0), axis=0
    )
    weights = jnp.asarray(WEIGHTS)
    weight_cube = weights[:, None, None] * weights[None, :, None] * weights[None, None, :]
    mass_cube = (
        jnp.take(mass_weights, inverse, axis=-1).reshape(8, 8, 8, height_count)
        * weight_cube[:, :, :, None]
    )
    flow = jnp.take(velocity, inverse, axis=-1).reshape(3, 8, 8, 8, height_count)
    fields_now = jnp.take(moment_fields, inverse, axis=-1).reshape(count, 8, 8, 8, height_count)
    adjoint_now = jnp.take(adjoint_fields, inverse, axis=-1).reshape(count, 8, 8, 8, height_count)
    table = jnp.asarray(shift_tables())
    out_f, out_a = fused(fields_now, adjoint_now, flow, mass_cube, table, diffusivity, ndev, cols)
    moments = jnp.take(out_f.reshape(count, 512, height_count), height, axis=-1)
    sensitivities = jnp.take(out_a.reshape(count, 512, height_count), height, axis=-1)
    return (moments, sensitivities)


def solution(mesh):
    in_specs = (
        P(None, None, "elem"),
        P(None, None, "elem"),
        P(None, None, "elem"),
        P(None, "elem"),
        P(),
        P("elem"),
    )
    out_specs = (P(None, None, "elem"), P(None, None, "elem"))
    return jax.shard_map(shards, mesh=mesh, in_specs=in_specs, out_specs=out_specs, check_vma=False)
```

time: 196 us -> 93.1 us (0.47); the launches traced: 192 us -> 92.9 us
  Pallas kernels: 0 us -> 63.8 us
  waiting for transfers between devices: 39.9 us -> 0 us
  local copies, waits for them, and re-layouts: 57 us -> 22.2 us
  starting transfers between devices: 34.4 us -> 0 us
  matrix products: 29.2 us -> 0 us
  other arithmetic: 29.1 us -> 6.16 us
    pallas_call x0 -> x1, Pallas kernels: none -> 63.8 us  [fused(): pl.pallas_call(functools.partial(kernel, ndev, cols), out_shape=(jax.Shap...]
    ppermute x20 -> x0, waiting for transfers between devices: 39.9 us -> none  [the longest x5 18.2 us: extended(): lax.ppermute(tail, axis, [(i, (i + 1) % count) for i in range(count)])]
    ppermute x20 -> x0, starting transfers between devices: 34.4 us -> none  [the longest x10 22.8 us: from_behind(): return lax.ppermute(block, axis, route)]
    dot_general x24 -> x0, matrix products: 29.2 us -> none  [the longest x4 5.98 us: transposed(): jnp.einsum('kp,gijke->gijpe', derivative, quantity, precision=highest)]
    scatter-add x13 -> x0, local copies, waits for them, and re-layouts: 16.3 us -> none  [the longest x4 6.66 us: assemble(): values = values.at[:, 7].add(row_high_ok * from_upper)]
    mul x10 -> x0, other arithmetic: 7.23 us -> none  [the longest x2 2.84 us: adjoint_terms(): mass_cube * (velocity[1] * quantity + scaled * gradients[1])]
    unnamed x83 -> x16, local copies, waits for them, and re-layouts: 12.5 us -> 5.85 us
    slice x22 -> x0, local copies, waits for them, and re-layouts: 6.1 us -> none  [the longest x1 1.78 us: forward_terms(): velocity[2] * gradients[2]]
  transfers between devices with their start and end apart: 20 -> 0, of which waited for: 12 -> 0; matrix products, arithmetic and copies ran while one was open for 36% -> 0% of each run, Pallas kernels for 0% -> 0%
where the time goes in v1:
time: 93.1 us; the launch traced here: 92.9 us
  Pallas kernels  63.8 us (69%)
  local copies, waits for them, and re-layouts  22.2 us (24%)
  other arithmetic  6.16 us (7%)
    pallas_call x1, Pallas kernels, fused(): pl.pallas_call(functools.partial(kernel, ndev, cols), out_shape=(jax.Shap...  63.8 us
    unnamed x16, local copies, waits for them, and re-layouts  5.85 us
    select_n x1, other arithmetic, shards(): jnp.take(velocity, inverse, axis=-1).reshape(3, 8, 8, 8, height_count)  2.61 us
    gather x1, local copies, waits for them, and re-layouts, shards(): jnp.take(adjoint_fields, inverse, axis=-1)  2.15 us
    gather x1, local copies, waits for them, and re-layouts, shards(): jnp.take(moment_fields, inverse, axis=-1)  2.12 us
    gather x1, local copies, waits for them, and re-layouts, shards(): jnp.take(out_a.reshape(count, 512, height_count), height, axis=-1)  2.09 us
    gather x1, local copies, waits for them, and re-layouts, shards(): jnp.take(velocity, inverse, axis=-1).reshape(3, 8, 8, 8, height_count)  2.09 us

profile of v1, /device:TPU:64, one launch (start us, length us, event | category | flops | bytes accessed | tf_op | source)
XLA Modules:
  0.0 92.9 jit_solution(2848838897244080517)
XLA Ops:
  0.6 0.7 compare_and_fusion
  1.3 0.1 select_reduce_fusion
  1.4 1.6 %copy.24 = f32[3,512,128]{1,0,2:T(4,128)S(1)} copy(f32[3,512,128]{2,1,0:T(8,128)} %param.10) | data formatting | bytes 1572864 | tf_op args[0]
  3.0 0.0 copy-start
  3.1 2.1 %gather_fusion.1 = f32[128,3,512]{2,1,0:T(4,128)} fusion(f32[3,512,128]{1,0,2:T(4,128)S(1)} %copy.24, s32[1024]{0:T(1024)S(1)} %pad_clamp_fusion.2), kind=kCustom, calls=%fused_computation.clone | custom fusion | bytes 1573376 | tf_op jit(solution)/shard_map/jit(_take)/gather | solution.py:333
  5.2 0.5 copy.26
  5.7 0.0 copy-start.1
  5.7 2.2 %gather_fusion.2 = f32[128,3,512]{2,1,0:T(4,128)} fusion(f32[3,512,128]{1,0,2:T(4,128)S(1)} %copy.26, s32[1024]{0:T(1024)S(1)} %pad_clamp_fusion.2), kind=kCustom, calls=%fused_computation.1.clone | custom fusion | bytes 1573376 | tf_op jit(solution)/shard_map/jit(_take)/gather | solution.py:334
  7.8 0.5 copy.28
  8.3 2.1 %gather_fusion.3 = f32[128,3,512]{2,1,0:T(4,128)} fusion(f32[3,512,128]{1,0,2:T(4,128)S(1)} %copy.28, s32[1024]{0:T(1024)S(1)} %pad_clamp_fusion.2), kind=kCustom, calls=%fused_computation.2.clone | custom fusion | bytes 1573376 | tf_op jit(solution)/shard_map/jit(_take)/gather | solution.py:332
  10.4 2.6 %select_bitcast_fusion.2 = (f32[3,512,128]{1,0,2:T(4,128)S(1)}, f32[3,512,128]{1,0,2:T(4,128)S(1)}, f32[3,512,128]{1,0,2:T(4,128)S(1)}) fusion(f32[128,3,512]{2,1,0:T(4,128)} %gather_fusion.3, pred[128]{0:T(512)(128)(4,1)S(1)} %compare_and_fusion.1, f32[128,3,512]{2,1,0:T(4,128)} %gather_fusion.2, f32[128,3,512]{2,1,0:T(4,128)} %gather_fusion.1), kind=kLoop, calls=%fused_computation.8 | loop fusion | flops 589824 | bytes 4718720 | tf_op jit(solution)/shard_map/jit(_take)/select_n | solution.py:332
  13.0 1.2 %copy.25 = f32[3,512,128]{2,1,0:T(8,128)} copy(f32[3,512,128]{1,0,2:T(4,128)S(1)} %get-tuple-element.17) | data formatting | bytes 1572864 | tf_op jit(solution)/shard_map/jit(_take)/select_n | solution.py:333
  14.3 1.2 %copy.27 = f32[3,512,128]{2,1,0:T(8,128)} copy(f32[3,512,128]{1,0,2:T(4,128)S(1)} %get-tuple-element.16) | data formatting | bytes 1572864 | tf_op jit(solution)/shard_map/jit(_take)/select_n | solution.py:334
  15.5 1.2 %copy.29 = f32[3,512,128]{2,1,0:T(8,128)} copy(f32[3,512,128]{1,0,2:T(4,128)S(1)} %get-tuple-element.15) | data formatting | bytes 1572864 | tf_op jit(solution)/shard_map/jit(_take)/select_n | solution.py:332
  16.8 0.0 copy-done.3
  16.8 0.1 copy.30
  16.9 0.8 gather_fusion
  17.7 0.1 copy.31
  17.8 0.0 copy-start.4
  17.8 0.6 copy-done.4
  18.5 0.1 broadcast_multiply_fusion.1
  18.5 0.1 broadcast_multiply_fusion
  18.6 0.9 select_multiply_fusion.mass_ref
  19.5 63.8 %shard_map.95 = (f32[3,8,8,8,128]{4,3,2,1,0:T(8,128)}, f32[3,8,8,8,128]{4,3,2,1,0:T(8,128)}) custom-call(f32[3,8,8,8,128]{4,3,2,1,0:T(8,128)} %bitcast.21, f32[3,8,8,8,128]{4,3,2,1,0:T(8,128)} %bitcast.22, f32[3,8,8,8,128]{4,3,2,1,0:T(8,128)} %bitcast.23, f32[8,8,8,128]{3,2,1,0:T(8,128)} %select_multiply_fusion.mass_ref, ...), custom_call_target="tpu_custom_call" | custom-call | tf_op jit(solution)/shard_map/pallas_call | solution.py:304
  83.2 1.6 %copy.32 = f32[3,512,128]{1,0,2:T(4,128)S(1)} copy(f32[3,512,128]{2,1,0:T(8,128)} %bitcast.27) | data formatting | bytes 1572864 | tf_op jit(solution)/shard_map/reshape | solution.py:337
  84.9 1.2 %gather_fusion.4 = f32[128,3,512]{2,1,0:T(4,128)S(1)} fusion(f32[3,512,128]{1,0,2:T(4,128)S(1)} %copy.32, s32[1024]{0:T(1024)S(1)} %pad_clamp_fusion), kind=kCustom, calls=%fused_computation.3.clone | custom fusion | bytes 1573376 | tf_op jit(solution)/shard_map/jit(_take)/gather | solution.py:337
  86.1 0.0 copy-done.2
  86.1 0.5 copy.33
  86.6 2.1 %gather_fusion.5 = f32[128,3,512]{2,1,0:T(4,128)} fusion(f32[3,512,128]{1,0,2:T(4,128)S(1)} %copy.33, s32[1024]{0:T(1024)S(1)} %pad_clamp_fusion), kind=kCustom, calls=%fused_computation.4.clone | custom fusion | bytes 1573376 | tf_op jit(solution)/shard_map/jit(_take)/gather | solution.py:338
  88.7 1.7 %select_bitcast_fusion = (f32[3,512,128]{1,0,2:T(4,128)S(1)}, f32[3,512,128]{1,0,2:T(4,128)S(1)}) fusion(f32[128,3,512]{2,1,0:T(4,128)} %gather_fusion.5, pred[128]{0:T(512)(128)(4,1)S(1)} %get-tuple-element.11, f32[128,3,512]{2,1,0:T(4,128)S(1)} %gather_fusion.4), kind=kLoop, calls=%fused_computation.6 | loop fusion | flops 393216 | bytes 3145856 | tf_op jit(solution)/shard_map/jit(_take)/select_n | solution.py:338
  90.4 1.2 %copy.34 = f32[3,512,128]{2,1,0:T(8,128)} copy(f32[3,512,128]{1,0,2:T(4,128)S(1)} %get-tuple-element.14) | data formatting | bytes 1572864
  91.6 1.2 %copy.35 = f32[3,512,128]{2,1,0:T(8,128)} copy(f32[3,512,128]{1,0,2:T(4,128)S(1)} %get-tuple-element.13) | data formatting | bytes 1572864
  (11 shorter events, 0.1 us)
Async XLA Ops:
  3.0 2.1 %copy-start = (f32[3,512,128]{2,1,0:T(8,128)S(1)}, f32[3,512,128]{2,1,0:T(8,128)}, u32[]{:S(2)}) copy-start(f32[3,512,128]{2,1,0:T(8,128)} %param.11) | copy-start | bytes 2359300
  5.7 2.2 %copy-start.1 = (f32[3,512,128]{2,1,0:T(8,128)S(1)}, f32[3,512,128]{2,1,0:T(8,128)}, u32[]{:S(2)}) copy-start(f32[3,512,128]{2,1,0:T(8,128)} %param.12) | copy-start | bytes 2359300
  15.5 1.3 %copy-start.3 = (f32[512,128]{1,0:T(8,128)S(1)}, f32[512,128]{1,0:T(8,128)}, u32[]{:S(2)}) copy-start(f32[512,128]{1,0:T(8,128)} %param.13) | copy-start | bytes 786436
  17.8 0.7 copy-start.4
  84.9 1.2 %copy-start.2 = (f32[3,8,8,8,128]{4,3,2,1,0:T(8,128)S(1)}, f32[3,8,8,8,128]{4,3,2,1,0:T(8,128)}, u32[]{:S(2)}) copy-start(f32[3,8,8,8,128]{4,3,2,1,0:T(8,128)} %get-tuple-element.6) | copy-start | bytes 2359300

commit v2 on v1

--- a/solution.py
+++ b/solution.py
@@ -136,15 +136,35 @@
     return v + jnp.where((sub == 7) & (lane < 127), above, zero)
 
 
+def permute(x, pm):
+    bf = jnp.bfloat16
+    f32 = jnp.float32
+    x1 = x.astype(bf)
+    r1 = x - x1.astype(f32)
+    x2 = r1.astype(bf)
+    x3 = (r1 - x2.astype(f32)).astype(bf)
+    y = jnp.dot(x1, pm, preferred_element_type=f32)
+    y = y + jnp.dot(x2, pm, preferred_element_type=f32)
+    return y + jnp.dot(x3, pm, preferred_element_type=f32)
+
+
 def kernel(
     ndev,
     cols,
+    fld_in,
+    adj_in,
+    vel_in,
+    mass_in,
+    tab_ref,
+    pin_ref,
+    pout_ref,
+    kap_ref,
+    out_f_in,
+    out_a_in,
     fld_ref,
     adj_ref,
     vel_ref,
     mass_ref,
-    tab_ref,
-    kap_ref,
     out_f_ref,
     out_a_ref,
     x1,
@@ -186,6 +206,15 @@
         pl.semaphore_signal(barrier, inc=1, device_id=(nb,), device_id_type=pl.DeviceIdType.MESH)
     pl.semaphore_wait(barrier, 4)
 
+    def sort_in(src_ref, dst_ref):
+        dst_ref[...] = permute(src_ref[...], pin_ref[...]).reshape(dst_ref.shape)
+
+    for f in range(3):
+        sort_in(fld_in.at[f], fld_ref.at[f])
+        sort_in(adj_in.at[f], adj_ref.at[f])
+        sort_in(vel_in.at[f], vel_ref.at[f])
+    sort_in(mass_in, mass_ref)
+
     def exchange(x, nf, rnd, sj, rj, si, ri):
         for f in range(nf):
             x[f] = z_assemble(x[f])
@@ -283,13 +312,23 @@
 
     lax.fori_loop(0, 3, a2_body, 0)
 
-
-def fused(fields, adjoint, flow, mass, table, kappa, ndev, cols):
+    for f in range(3):
+        out_f_in[f] = permute(out_f_ref[f].reshape(512, 128), pout_ref[...])
+        out_a_in[f] = permute(out_a_ref[f].reshape(512, 128), pout_ref[...])
+
+
+def fused(fields, adjoint, flow, mass, table, p_in, p_out, kappa, ndev, cols):
     cube = (8, 8, 8, 128)
     f32 = jnp.float32
     vmem = pl.BlockSpec(memory_space=pltpu.VMEM)
     smem = pl.BlockSpec(memory_space=pltpu.SMEM)
     scratch = [
+        pltpu.VMEM((3,) + cube, f32),
+        pltpu.VMEM((3,) + cube, f32),
+        pltpu.VMEM((3,) + cube, f32),
+        pltpu.VMEM(cube, f32),
+        pltpu.VMEM((3,) + cube, f32),
+        pltpu.VMEM((3,) + cube, f32),
         pltpu.VMEM((4,) + cube, f32),
         pltpu.VMEM((6,) + cube, f32),
         pltpu.VMEM((3,) + cube, f32),
@@ -301,42 +340,32 @@
         for _ in range(4):
             scratch.append(pltpu.VMEM((2, nf, 8, 8, 128), f32))
     scratch += [pltpu.SemaphoreType.DMA((3, 2, 2)), pltpu.SemaphoreType.DMA((3, 2, 2))]
+    shape = fields.shape
     return pl.pallas_call(
         functools.partial(kernel, ndev, cols),
-        out_shape=(jax.ShapeDtypeStruct((3,) + cube, f32), jax.ShapeDtypeStruct((3,) + cube, f32)),
-        in_specs=[vmem, vmem, vmem, vmem, vmem, smem],
+        out_shape=(jax.ShapeDtypeStruct(shape, f32), jax.ShapeDtypeStruct(shape, f32)),
+        in_specs=[vmem, vmem, vmem, vmem, vmem, vmem, vmem, smem],
         out_specs=(vmem, vmem),
         scratch_shapes=scratch,
         compiler_params=pltpu.CompilerParams(
             collective_id=0, has_side_effects=True, vmem_limit_bytes=60 * 1024 * 1024
         ),
-    )(fields, adjoint, flow, mass, table, kappa)
+    )(fields, adjoint, flow, mass, table, p_in, p_out, kappa)
 
 
 def shards(moment_fields, adjoint_fields, velocity, mass_weights, diffusivity, numbering):
     height_count = numbering.shape[0]
-    count = moment_fields.shape[0]
     ndev = lax.axis_size("elem")
     cols = ndev // DA
     height = numbering % height_count
     slot_index = lax.iota(jnp.int32, height_count)
-    inverse = jnp.sum(
-        jnp.where(height[:, None] == slot_index[None, :], slot_index[:, None], 0), axis=0
-    )
+    p_in = (height[:, None] == slot_index[None, :]).astype(jnp.bfloat16)
+    p_out = (slot_index[:, None] == height[None, :]).astype(jnp.bfloat16)
     weights = jnp.asarray(WEIGHTS)
-    weight_cube = weights[:, None, None] * weights[None, :, None] * weights[None, None, :]
-    mass_cube = (
-        jnp.take(mass_weights, inverse, axis=-1).reshape(8, 8, 8, height_count)
-        * weight_cube[:, :, :, None]
-    )
-    flow = jnp.take(velocity, inverse, axis=-1).reshape(3, 8, 8, 8, height_count)
-    fields_now = jnp.take(moment_fields, inverse, axis=-1).reshape(count, 8, 8, 8, height_count)
-    adjoint_now = jnp.take(adjoint_fields, inverse, axis=-1).reshape(count, 8, 8, 8, height_count)
+    weight_cube = (weights[:, None, None] * weights[None, :, None] * weights[None, None, :]).reshape(512, 1)
+    mass_cube = mass_weights * weight_cube
     table = jnp.asarray(shift_tables())
-    out_f, out_a = fused(fields_now, adjoint_now, flow, mass_cube, table, diffusivity, ndev, cols)
-    moments = jnp.take(out_f.reshape(count, 512, height_count), height, axis=-1)
-    sensitivities = jnp.take(out_a.reshape(count, 512, height_count), height, axis=-1)
-    return (moments, sensitivities)
+    return fused(moment_fields, adjoint_fields, velocity, mass_cube, table, p_in, p_out, diffusivity, ndev, cols)
 
 
 def solution(mesh):

time: 93.1 us -> 73 us (0.78)
  local copies, waits for them, and re-layouts: 22.2 us -> 3.12 us
  other arithmetic: 6.16 us -> 3.29 us
  Pallas kernels: 63.8 us -> 65.8 us
    gather x7 -> x0, local copies, waits for them, and re-layouts: 10.5 us -> none  [the longest x1 2.15 us: shards(): jnp.take(adjoint_fields, inverse, axis=-1)]
    select_n x5 -> x1, other arithmetic: 4.37 us -> 0.67 us  [shards(): height = numbering % height_count]
    select_n x3 -> x0, local copies, waits for them, and re-layouts: 3.7 us -> none  [the longest x1 1.24 us: shards(): jnp.take(velocity, inverse, axis=-1).reshape(3, 8, 8, 8, height_count)]
    unnamed x16 -> x6, local copies, waits for them, and re-layouts: 5.85 us -> 3.03 us
    reshape x2 -> x0, local copies, waits for them, and re-layouts: 2.11 us -> none  [the longest x1 1.62 us: shards(): moments = jnp.take(out_f.reshape(count, 512, height_count), height, axis=-1)]
    pallas_call x1, Pallas kernels: 63.8 us -> 65.8 us  [fused(): pl.pallas_call(functools.partial(kernel, ndev, cols), out_shape=(jax.Shap...]
    mul x1, other arithmetic: 0.85 us -> 1.79 us  [shards(): mass_cube = mass_weights * weight_cube]
where the time goes in v2:
time: 73 us; the launch traced here: 72.9 us
  Pallas kernels  65.8 us (90%)
  other arithmetic  3.29 us (5%)
  local copies, waits for them, and re-layouts  3.12 us (4%)
    pallas_call x1, Pallas kernels, fused(): pl.pallas_call(functools.partial(kernel, ndev, cols), out_shape=(jax.Shap...  65.8 us
    unnamed x6, local copies, waits for them, and re-layouts  3.03 us
    mul x1, other arithmetic, shards(): mass_cube = mass_weights * weight_cube  1.79 us

profile of v2, /device:TPU:64, one launch (start us, length us, event | category | flops | bytes accessed | tf_op | source)
XLA Modules:
  0.0 72.9 jit_solution(15582524736515943139)
XLA Ops:
  0.6 0.0 copy-start.1
  0.6 0.7 and_select_fusion
  1.3 0.0 copy-done.1
  1.3 0.1 broadcast_multiply_fusion.2
  1.4 0.1 broadcast_multiply_fusion.1
  1.5 0.1 mul.52
  1.6 0.7 fusion.1
  2.2 1.8 %broadcast_multiply_fusion.mass_in = f32[512,128]{1,0:T(8,128)} fusion(f32[512,128]{1,0:T(8,128)} %param.11, f32[512]{0:T(512)S(1)} %mul.52), kind=kLoop, calls=%fused_computation | loop fusion | flops 65536 | bytes 526336 | tf_op jit(solution)/shard_map/mul | solution.py:366
  4.0 65.8 %shard_map.95 = (f32[3,512,128]{2,1,0:T(8,128)}, f32[3,512,128]{2,1,0:T(8,128)}) custom-call(f32[3,512,128]{2,1,0:T(8,128)} %fld_in.1, f32[3,512,128]{2,1,0:T(8,128)} %adj_in.1, f32[3,512,128]{2,1,0:T(8,128)} %vel_in.1, f32[512,128]{1,0:T(8,128)} %broadcast_multiply_fusion.mass_in, f32[16,8,128]{2,1,0:T(8,128)} %constant.20.clone.tab_ref, ...), custom_call_target="tpu_custom_call" | custom-call | tf_op jit(solution)/shard_map/pallas_call | solution.py:344
  69.8 0.0 copy-start
  69.8 2.1 %copy.12 = f32[3,512,128]{2,1,0:T(8,128)} copy(f32[3,512,128]{2,1,0:T(8,128)} %get-tuple-element.6) | data formatting | bytes 1572864
  72.0 0.0 copy-done
  72.0 0.9 %copy.13 = f32[3,512,128]{2,1,0:T(8,128)} copy(f32[3,512,128]{2,1,0:T(8,128)S(1)} %copy-done) | data formatting | bytes 1572864
Async XLA Ops:
  0.6 0.7 copy-start.1
  69.8 2.1 %copy-start = (f32[3,512,128]{2,1,0:T(8,128)S(1)}, f32[3,512,128]{2,1,0:T(8,128)}, u32[]{:S(2)}) copy-start(f32[3,512,128]{2,1,0:T(8,128)} %get-tuple-element.7) | copy-start | bytes 2359300

commit v3 on v2

--- a/solution.py
+++ b/solution.py
@@ -167,24 +167,14 @@
     mass_ref,
     out_f_ref,
     out_a_ref,
-    x1,
-    x2,
-    x3,
     ms_ref,
     f1_ref,
     a1_ref,
-    sj1,
-    rj1,
-    si1,
-    ri1,
-    sj2,
-    rj2,
-    si2,
-    ri2,
-    sj3,
-    rj3,
-    si3,
-    ri3,
+    xs,
+    sj,
+    rj,
+    si,
+    ri,
     ssem,
     rsem,
 ):
@@ -215,102 +205,134 @@
         sort_in(vel_in.at[f], vel_ref.at[f])
     sort_in(mass_in, mass_ref)
 
-    def exchange(x, nf, rnd, sj, rj, si, ri):
-        for f in range(nf):
-            x[f] = z_assemble(x[f])
-        for f in range(nf):
-            sj[0, f] = x[f, :, 0]
-            sj[1, f] = x[f, :, 7]
-
-        def pair(s_buf, r_buf, d, hi, lo, has_hi, has_lo, fixup):
-            c_hi = pltpu.make_async_remote_copy(
-                s_buf.at[1], r_buf.at[0], ssem.at[rnd, d, 1], rsem.at[rnd, d, 0],
-                device_id=(hi,), device_id_type=pl.DeviceIdType.MESH,
-            )
-            c_lo = pltpu.make_async_remote_copy(
-                s_buf.at[0], r_buf.at[1], ssem.at[rnd, d, 0], rsem.at[rnd, d, 1],
-                device_id=(lo,), device_id_type=pl.DeviceIdType.MESH,
-            )
-
-            @pl.when(has_hi)
-            def _():
-                c_hi.start()
-
-            @pl.when(has_lo)
-            def _():
-                c_lo.start()
-
-            @pl.when(has_hi)
-            def _():
-                c_hi.wait_send()
-                c_lo.wait_recv()
-                fixup(7, r_buf.at[1])
-
-            @pl.when(has_lo)
-            def _():
-                c_lo.wait_send()
-                c_hi.wait_recv()
-                fixup(0, r_buf.at[0])
-
-        def fix_j(side, buf):
-            for f in range(nf):
-                x[f, :, side] = x[f, :, side] + buf[f]
-
-        pair(sj, rj, 0, right, left, has_right, has_left, fix_j)
-
-        for f in range(nf):
-            si[0, f] = x[f, 0]
-            si[1, f] = x[f, 7]
-
-        def fix_i(side, buf):
-            for f in range(nf):
-                x[f, side] = x[f, side] + buf[f]
-
-        pair(si, ri, 1, up, down, has_up, has_down, fix_i)
+    links = (
+        (sj, rj, right, left, has_right, has_left),
+        (si, ri, up, down, has_up, has_down),
+    )
+
+    def copies(u, d):
+        s_buf, r_buf, hi, lo = links[d][:4]
+        c_hi = pltpu.make_async_remote_copy(
+            s_buf.at[u, 1], r_buf.at[u, 0], ssem.at[u, d, 1], rsem.at[u, d, 0],
+            device_id=(hi,), device_id_type=pl.DeviceIdType.MESH,
+        )
+        c_lo = pltpu.make_async_remote_copy(
+            s_buf.at[u, 0], r_buf.at[u, 1], ssem.at[u, d, 0], rsem.at[u, d, 1],
+            device_id=(lo,), device_id_type=pl.DeviceIdType.MESH,
+        )
+        return c_hi, c_lo
+
+    def face(u, d, side):
+        return xs.at[u, :, side] if d == 0 else xs.at[u, side]
+
+    def send(u, d):
+        s_buf = links[d][0]
+        s_buf[u, 0] = face(u, d, 0)[...]
+        s_buf[u, 1] = face(u, d, 7)[...]
+        c_hi, c_lo = copies(u, d)
+        has_hi, has_lo = links[d][4:]
+
+        @pl.when(has_hi)
+        def _():
+            c_hi.start()
+
+        @pl.when(has_lo)
+        def _():
+            c_lo.start()
+
+    def finish(u, d):
+        r_buf = links[d][1]
+        c_hi, c_lo = copies(u, d)
+        has_hi, has_lo = links[d][4:]
+
+        @pl.when(has_hi)
+        def _():
+            c_hi.wait_send()
+            c_lo.wait_recv()
+            top = face(u, d, 7)
+            top[...] = top[...] + r_buf[u, 1]
+
+        @pl.when(has_lo)
+        def _():
+            c_lo.wait_send()
+            c_hi.wait_recv()
+            bottom = face(u, d, 0)
+            bottom[...] = bottom[...] + r_buf[u, 0]
+
+    class Unit:
+        def __init__(self, u, done):
+            self.u = u
+            self.stage = 0
+            self.done = done
+            xs[u] = z_assemble(xs[u])
+            send(u, 0)
+
+        def advance(self):
+            finish(self.u, self.stage)
+            if self.stage == 0:
+                send(self.u, 1)
+                self.stage = 1
+                return False
+            self.done()
+            return True
 
     def flow():
         return (vel_ref[0], vel_ref[1], vel_ref[2])
 
-    x1[0] = mass_ref[...]
-
-    def r1_body(f, c):
-        x1[f + 1] = forward_terms(fld_ref[f], flow(), mass_ref[...], kap_ref[f], tab_ref)
-        return c
-
-    lax.fori_loop(0, 3, r1_body, 0)
-    exchange(x1, 4, 0, sj1, rj1, si1, ri1)
-    ms_ref[...] = x1[0]
-
-    def f1_body(f, c):
-        f1_ref[f] = fld_ref[f] + time_step * x1[f + 1] / ms_ref[...]
-        x2[f + 3] = adj_ref[f] / ms_ref[...]
-        return c
-
-    lax.fori_loop(0, 3, f1_body, 0)
-
-    def r2_body(f, c):
-        x2[f] = forward_terms(f1_ref[f], flow(), mass_ref[...], kap_ref[f], tab_ref)
-        return c
-
-    lax.fori_loop(0, 3, r2_body, 0)
-    exchange(x2, 6, 1, sj2, rj2, si2, ri2)
-
-    def a1_body(f, c):
-        out_f_ref[f] = f1_ref[f] + time_step * x2[f] / ms_ref[...]
-        a1 = adj_ref[f] + time_step * adjoint_terms(x2[f + 3], flow(), mass_ref[...], kap_ref[f], tab_ref)
+    ready = []
+    fresh = []
+    state = {"ms": False}
+
+    def mass_done():
+        ms_ref[...] = xs[0]
+        state["ms"] = True
+        for f in range(3):
+            xs[7 + f] = adj_ref[f] / ms_ref[...]
+            fresh.append(Unit(7 + f, functools.partial(adjoint_first_done, f)))
+
+    def forward_first(f):
+        xs[1 + f] = forward_terms(fld_ref[f], flow(), mass_ref[...], kap_ref[f], tab_ref)
+        fresh.append(Unit(1 + f, functools.partial(forward_first_done, f)))
+
+    def forward_first_done(f):
+        assert state["ms"]
+        f1_ref[f] = fld_ref[f] + time_step * xs[1 + f] / ms_ref[...]
+        ready.append(functools.partial(forward_second, f))
+
+    def forward_second(f):
+        xs[4 + f] = forward_terms(f1_ref[f], flow(), mass_ref[...], kap_ref[f], tab_ref)
+        fresh.append(Unit(4 + f, functools.partial(forward_second_done, f)))
+
+    def forward_second_done(f):
+        out_f_ref[f] = f1_ref[f] + time_step * xs[4 + f] / ms_ref[...]
+
+    def adjoint_first_done(f):
+        ready.append(functools.partial(adjoint_second, f))
+
+    def adjoint_second(f):
+        a1 = adj_ref[f] + time_step * adjoint_terms(xs[7 + f], flow(), mass_ref[...], kap_ref[f], tab_ref)
         a1_ref[f] = a1
-        x3[f] = a1 / ms_ref[...]
-        return c
-
-    lax.fori_loop(0, 3, a1_body, 0)
-
-    exchange(x3, 3, 2, sj3, rj3, si3, ri3)
-
-    def a2_body(f, c):
-        out_a_ref[f] = a1_ref[f] + time_step * adjoint_terms(x3[f], flow(), mass_ref[...], kap_ref[f], tab_ref)
-        return c
-
-    lax.fori_loop(0, 3, a2_body, 0)
+        xs[10 + f] = a1 / ms_ref[...]
+        fresh.append(Unit(10 + f, functools.partial(adjoint_second_done, f)))
+
+    def adjoint_second_done(f):
+        ready.append(functools.partial(adjoint_third, f))
+
+    def adjoint_third(f):
+        out_a_ref[f] = a1_ref[f] + time_step * adjoint_terms(xs[10 + f], flow(), mass_ref[...], kap_ref[f], tab_ref)
+
+    xs[0] = mass_ref[...]
+    pending = [Unit(0, mass_done)]
+    for f in range(3):
+        ready.append(functools.partial(forward_first, f))
+    while ready or pending or fresh:
+        if ready:
+            ready.pop(0)()
+        for unit in list(pending):
+            if unit.advance():
+                pending.remove(unit)
+        pending += fresh
+        fresh.clear()
 
     for f in range(3):
         out_f_in[f] = permute(out_f_ref[f].reshape(512, 128), pout_ref[...])
@@ -320,6 +342,7 @@
 def fused(fields, adjoint, flow, mass, table, p_in, p_out, kappa, ndev, cols):
     cube = (8, 8, 8, 128)
     f32 = jnp.float32
+    units = 13
     vmem = pl.BlockSpec(memory_space=pltpu.VMEM)
     smem = pl.BlockSpec(memory_space=pltpu.SMEM)
     scratch = [
@@ -329,17 +352,14 @@
         pltpu.VMEM(cube, f32),
         pltpu.VMEM((3,) + cube, f32),
         pltpu.VMEM((3,) + cube, f32),
-        pltpu.VMEM((4,) + cube, f32),
-        pltpu.VMEM((6,) + cube, f32),
-        pltpu.VMEM((3,) + cube, f32),
         pltpu.VMEM(cube, f32),
         pltpu.VMEM((3,) + cube, f32),
         pltpu.VMEM((3,) + cube, f32),
+        pltpu.VMEM((units,) + cube, f32),
     ]
-    for nf in (4, 6, 3):
-        for _ in range(4):
-            scratch.append(pltpu.VMEM((2, nf, 8, 8, 128), f32))
-    scratch += [pltpu.SemaphoreType.DMA((3, 2, 2)), pltpu.SemaphoreType.DMA((3, 2, 2))]
+    for _ in range(4):
+        scratch.append(pltpu.VMEM((units, 2, 8, 8, 128), f32))
+    scratch += [pltpu.SemaphoreType.DMA((units, 2, 2)), pltpu.SemaphoreType.DMA((units, 2, 2))]
     shape = fields.shape
     return pl.pallas_call(
         functools.partial(kernel, ndev, cols),

time: 73 us -> 72.1 us (0.988)
  Pallas kernels: 65.8 us -> 64.8 us
    pallas_call x1, Pallas kernels: 65.8 us -> 64.8 us  [fused(): pl.pallas_call(functools.partial(kernel, ndev, cols), out_shape=(jax.Shap...]
where the time goes in v3:
time: 72.1 us; the launch traced here: 71.9 us
  Pallas kernels  64.8 us (90%)
  other arithmetic  3.29 us (5%)
  local copies, waits for them, and re-layouts  3.12 us (4%)
    pallas_call x1, Pallas kernels, fused(): pl.pallas_call(functools.partial(kernel, ndev, cols), out_shape=(jax.Shap...  64.8 us
    unnamed x6, local copies, waits for them, and re-layouts  3.03 us
    mul x1, other arithmetic, shards(): mass_cube = mass_weights * weight_cube  1.79 us

profile of v3, /device:TPU:64, one launch (start us, length us, event | category | flops | bytes accessed | tf_op | source)
XLA Modules:
  0.0 71.9 jit_solution(14497035768075901768)
XLA Ops:
  0.6 0.0 copy-start.1
  0.6 0.7 and_select_fusion
  1.3 0.0 copy-done.1
  1.3 0.1 broadcast_multiply_fusion.2
  1.4 0.1 broadcast_multiply_fusion.1
  1.5 0.1 mul.52
  1.6 0.7 fusion.1
  2.2 1.8 %broadcast_multiply_fusion.mass_in = f32[512,128]{1,0:T(8,128)} fusion(f32[512,128]{1,0:T(8,128)} %param.11, f32[512]{0:T(512)S(1)} %mul.52), kind=kLoop, calls=%fused_computation | loop fusion | flops 65536 | bytes 526336 | tf_op jit(solution)/shard_map/mul | solution.py:386
  4.0 64.8 %shard_map.95 = (f32[3,512,128]{2,1,0:T(8,128)}, f32[3,512,128]{2,1,0:T(8,128)}) custom-call(f32[3,512,128]{2,1,0:T(8,128)} %fld_in.1, f32[3,512,128]{2,1,0:T(8,128)} %adj_in.1, f32[3,512,128]{2,1,0:T(8,128)} %vel_in.1, f32[512,128]{1,0:T(8,128)} %broadcast_multiply_fusion.mass_in, f32[16,8,128]{2,1,0:T(8,128)} %constant.20.clone.tab_ref, ...), custom_call_target="tpu_custom_call" | custom-call | tf_op jit(solution)/shard_map/pallas_call | solution.py:364
  68.8 0.0 copy-start
  68.9 2.1 %copy.12 = f32[3,512,128]{2,1,0:T(8,128)} copy(f32[3,512,128]{2,1,0:T(8,128)} %get-tuple-element.6) | data formatting | bytes 1572864
  71.0 0.0 copy-done
  71.0 0.9 %copy.13 = f32[3,512,128]{2,1,0:T(8,128)} copy(f32[3,512,128]{2,1,0:T(8,128)S(1)} %copy-done) | data formatting | bytes 1572864
Async XLA Ops:
  0.6 0.7 copy-start.1
  68.8 2.1 %copy-start = (f32[3,512,128]{2,1,0:T(8,128)S(1)}, f32[3,512,128]{2,1,0:T(8,128)}, u32[]{:S(2)}) copy-start(f32[3,512,128]{2,1,0:T(8,128)} %get-tuple-element.7) | copy-start | bytes 2359300

commit v4 on v3

--- a/solution.py
+++ b/solution.py
@@ -175,6 +175,8 @@
     rj,
     si,
     ri,
+    sd,
+    rd,
     ssem,
     rsem,
 ):
@@ -191,10 +193,15 @@
     has_up = row < DA - 1
     has_down = row > 0
 
+    up_right = (me + cols + 1) % ndev
+    up_left = (me + cols + ndev - 1) % ndev
+    down_right = (me + 2 * ndev - cols + 1) % ndev
+    down_left = (me + 2 * ndev - cols - 1) % ndev
+
     barrier = pltpu.get_barrier_semaphore()
-    for nb in (left, right, up, down):
+    for nb in (left, right, up, down, up_right, up_left, down_right, down_left):
         pl.semaphore_signal(barrier, inc=1, device_id=(nb,), device_id_type=pl.DeviceIdType.MESH)
-    pl.semaphore_wait(barrier, 4)
+    pl.semaphore_wait(barrier, 8)
 
     def sort_in(src_ref, dst_ref):
         dst_ref[...] = permute(src_ref[...], pin_ref[...]).reshape(dst_ref.shape)
@@ -205,134 +212,105 @@
         sort_in(vel_in.at[f], vel_ref.at[f])
     sort_in(mass_in, mass_ref)
 
-    links = (
-        (sj, rj, right, left, has_right, has_left),
-        (si, ri, up, down, has_up, has_down),
-    )
-
-    def copies(u, d):
-        s_buf, r_buf, hi, lo = links[d][:4]
-        c_hi = pltpu.make_async_remote_copy(
-            s_buf.at[u, 1], r_buf.at[u, 0], ssem.at[u, d, 1], rsem.at[u, d, 0],
-            device_id=(hi,), device_id_type=pl.DeviceIdType.MESH,
-        )
-        c_lo = pltpu.make_async_remote_copy(
-            s_buf.at[u, 0], r_buf.at[u, 1], ssem.at[u, d, 0], rsem.at[u, d, 1],
-            device_id=(lo,), device_id_type=pl.DeviceIdType.MESH,
-        )
-        return c_hi, c_lo
-
-    def face(u, d, side):
-        return xs.at[u, :, side] if d == 0 else xs.at[u, side]
-
-    def send(u, d):
-        s_buf = links[d][0]
-        s_buf[u, 0] = face(u, d, 0)[...]
-        s_buf[u, 1] = face(u, d, 7)[...]
-        c_hi, c_lo = copies(u, d)
-        has_hi, has_lo = links[d][4:]
-
-        @pl.when(has_hi)
-        def _():
-            c_hi.start()
-
-        @pl.when(has_lo)
-        def _():
-            c_lo.start()
-
-    def finish(u, d):
-        r_buf = links[d][1]
-        c_hi, c_lo = copies(u, d)
-        has_hi, has_lo = links[d][4:]
-
-        @pl.when(has_hi)
-        def _():
-            c_hi.wait_send()
-            c_lo.wait_recv()
-            top = face(u, d, 7)
-            top[...] = top[...] + r_buf[u, 1]
-
-        @pl.when(has_lo)
-        def _():
-            c_lo.wait_send()
-            c_hi.wait_recv()
-            bottom = face(u, d, 0)
-            bottom[...] = bottom[...] + r_buf[u, 0]
-
-    class Unit:
-        def __init__(self, u, done):
-            self.u = u
-            self.stage = 0
-            self.done = done
-            xs[u] = z_assemble(xs[u])
-            send(u, 0)
-
-        def advance(self):
-            finish(self.u, self.stage)
-            if self.stage == 0:
-                send(self.u, 1)
-                self.stage = 1
-                return False
-            self.done()
-            return True
+    def plan(u):
+        face_j = lambda side: xs.at[u, :, side]
+        face_i = lambda side: xs.at[u, side]
+        sends = [
+            (sj.at[u, 1], rj.at[u, 0], right, has_right),
+            (sj.at[u, 0], rj.at[u, 1], left, has_left),
+            (si.at[u, 1], ri.at[u, 0], up, has_up),
+            (si.at[u, 0], ri.at[u, 1], down, has_down),
+            (sd.at[u, 0], rd.at[u, 0], up_right, has_up & has_right),
+            (sd.at[u, 1], rd.at[u, 1], up_left, has_up & has_left),
+            (sd.at[u, 2], rd.at[u, 2], down_right, has_down & has_right),
+            (sd.at[u, 3], rd.at[u, 3], down_left, has_down & has_left),
+        ]
+        copies = [
+            pltpu.make_async_remote_copy(
+                s, d, ssem.at[u, k], rsem.at[u, k], device_id=(t,), device_id_type=pl.DeviceIdType.MESH
+            )
+            for k, (s, d, t, _) in enumerate(sends)
+        ]
+        recv_has = [has_left, has_right, has_down, has_up,
+                    has_down & has_left, has_down & has_right, has_up & has_left, has_up & has_right]
+        targets = [
+            face_j(0), face_j(7), face_i(0), face_i(7),
+            xs.at[u, 0, 0], xs.at[u, 0, 7], xs.at[u, 7, 0], xs.at[u, 7, 7],
+        ]
+        return sends, copies, recv_has, targets
+
+    def start_unit(u):
+        xs[u] = z_assemble(xs[u])
+        sj[u, 0] = xs[u, :, 0]
+        sj[u, 1] = xs[u, :, 7]
+        si[u, 0] = xs[u, 0]
+        si[u, 1] = xs[u, 7]
+        sd[u, 0] = xs[u, 7, 7]
+        sd[u, 1] = xs[u, 7, 0]
+        sd[u, 2] = xs[u, 0, 7]
+        sd[u, 3] = xs[u, 0, 0]
+        sends, copies, _, _ = plan(u)
+        for (_, _, _, has), c in zip(sends, copies):
+            @pl.when(has)
+            def _():
+                c.start()
+
+    def finish_unit(u):
+        sends, copies, recv_has, targets = plan(u)
+        for (_, _, _, has), c in zip(sends, copies):
+            @pl.when(has)
+            def _():
+                c.wait_send()
+        for k in range(8):
+            @pl.when(recv_has[k])
+            def _():
+                copies[k].wait_recv()
+                targets[k][...] = targets[k][...] + sends[k][1][...]
 
     def flow():
         return (vel_ref[0], vel_ref[1], vel_ref[2])
 
-    ready = []
-    fresh = []
-    state = {"ms": False}
-
-    def mass_done():
-        ms_ref[...] = xs[0]
-        state["ms"] = True
-        for f in range(3):
-            xs[7 + f] = adj_ref[f] / ms_ref[...]
-            fresh.append(Unit(7 + f, functools.partial(adjoint_first_done, f)))
-
     def forward_first(f):
         xs[1 + f] = forward_terms(fld_ref[f], flow(), mass_ref[...], kap_ref[f], tab_ref)
-        fresh.append(Unit(1 + f, functools.partial(forward_first_done, f)))
-
-    def forward_first_done(f):
-        assert state["ms"]
-        f1_ref[f] = fld_ref[f] + time_step * xs[1 + f] / ms_ref[...]
-        ready.append(functools.partial(forward_second, f))
+        start_unit(1 + f)
 
     def forward_second(f):
-        xs[4 + f] = forward_terms(f1_ref[f], flow(), mass_ref[...], kap_ref[f], tab_ref)
-        fresh.append(Unit(4 + f, functools.partial(forward_second_done, f)))
-
-    def forward_second_done(f):
-        out_f_ref[f] = f1_ref[f] + time_step * xs[4 + f] / ms_ref[...]
-
-    def adjoint_first_done(f):
-        ready.append(functools.partial(adjoint_second, f))
+        finish_unit(1 + f)
+        f1 = fld_ref[f] + time_step * xs[1 + f] / ms_ref[...]
+        f1_ref[f] = f1
+        xs[4 + f] = forward_terms(f1, flow(), mass_ref[...], kap_ref[f], tab_ref)
+        start_unit(4 + f)
 
     def adjoint_second(f):
+        finish_unit(7 + f)
         a1 = adj_ref[f] + time_step * adjoint_terms(xs[7 + f], flow(), mass_ref[...], kap_ref[f], tab_ref)
         a1_ref[f] = a1
         xs[10 + f] = a1 / ms_ref[...]
-        fresh.append(Unit(10 + f, functools.partial(adjoint_second_done, f)))
-
-    def adjoint_second_done(f):
-        ready.append(functools.partial(adjoint_third, f))
+        start_unit(10 + f)
 
     def adjoint_third(f):
+        finish_unit(10 + f)
         out_a_ref[f] = a1_ref[f] + time_step * adjoint_terms(xs[10 + f], flow(), mass_ref[...], kap_ref[f], tab_ref)
 
     xs[0] = mass_ref[...]
-    pending = [Unit(0, mass_done)]
-    for f in range(3):
-        ready.append(functools.partial(forward_first, f))
-    while ready or pending or fresh:
-        if ready:
-            ready.pop(0)()
-        for unit in list(pending):
-            if unit.advance():
-                pending.remove(unit)
-        pending += fresh
-        fresh.clear()
+    start_unit(0)
+    forward_first(0)
+    forward_first(1)
+    finish_unit(0)
+    ms_ref[...] = xs[0]
+    for f in range(3):
+        xs[7 + f] = adj_ref[f] / ms_ref[...]
+        start_unit(7 + f)
+    forward_first(2)
+    for f in range(3):
+        forward_second(f)
+    for f in range(3):
+        adjoint_second(f)
+    for f in range(3):
+        adjoint_third(f)
+    for f in range(3):
+        finish_unit(4 + f)
+        out_f_ref[f] = f1_ref[f] + time_step * xs[4 + f] / ms_ref[...]
 
     for f in range(3):
         out_f_in[f] = permute(out_f_ref[f].reshape(512, 128), pout_ref[...])
@@ -359,7 +337,9 @@
     ]
     for _ in range(4):
         scratch.append(pltpu.VMEM((units, 2, 8, 8, 128), f32))
-    scratch += [pltpu.SemaphoreType.DMA((units, 2, 2)), pltpu.SemaphoreType.DMA((units, 2, 2))]
+    for _ in range(2):
+        scratch.append(pltpu.VMEM((units, 4, 8, 128), f32))
+    scratch += [pltpu.SemaphoreType.DMA((units, 8)), pltpu.SemaphoreType.DMA((units, 8))]
     shape = fields.shape
     return pl.pallas_call(
         functools.partial(kernel, ndev, cols),

time: 72.1 us -> 60.5 us (0.84)
  the two profiles are of different devices: /device:TPU:64 before, /device:TPU:63 now
where the time goes in v4:
time: 60.5 us; the launch traced here: 60.3 us
  Pallas kernels  53.2 us (88%)
  other arithmetic  3.29 us (5%)
  local copies, waits for them, and re-layouts  3.12 us (5%)
  between operations  0.66 us (1%)
    pallas_call x1, Pallas kernels, fused(): pl.pallas_call(functools.partial(kernel, ndev, cols), out_shape=(jax.Shap...  53.2 us
    unnamed x6, local copies, waits for them, and re-layouts  3.03 us
    mul x1, other arithmetic, shards(): mass_cube = mass_weights * weight_cube  1.79 us

profile of v4, /device:TPU:63, one launch (start us, length us, event | category | flops | bytes accessed | tf_op | source)
XLA Modules:
  0.0 60.3 jit_solution(3763966964398132783)
XLA Ops:
  0.6 0.0 copy-start.1
  0.6 0.7 %and_select_fusion = s32[128]{0:T(128)S(1)} fusion(s32[128]{0:T(128)} %param.13), kind=kLoop, calls=%fused_computation.9 | loop fusion | flops 1408 | bytes 1024 | tf_op jit(solution)/shard_map/jit(remainder)/select_n | solution.py:360
  1.3 0.0 copy-done.1
  1.3 0.1 broadcast_multiply_fusion.2
  1.4 0.1 broadcast_multiply_fusion.1
  1.5 0.1 mul.52
  1.6 0.7 %fusion.1 = (bf16[128,128]{1,0:T(8,128)(2,1)}, bf16[128,128]{1,0:T(8,128)(2,1)}) fusion(s32[128]{0:T(128)S(1)} %and_select_fusion), kind=kLoop, calls=%fused_computation.4 | loop fusion | flops 65536 | bytes 66048 | tf_op jit(solution)/shard_map/convert_element_type | solution.py:363
  2.2 1.8 %broadcast_multiply_fusion.mass_in = f32[512,128]{1,0:T(8,128)} fusion(f32[512,128]{1,0:T(8,128)} %param.11, f32[512]{0:T(512)S(1)} %mul.52), kind=kLoop, calls=%fused_computation | loop fusion | flops 65536 | bytes 526336 | tf_op jit(solution)/shard_map/mul | solution.py:366
  4.0 53.2 %shard_map.95 = (f32[3,512,128]{2,1,0:T(8,128)}, f32[3,512,128]{2,1,0:T(8,128)}) custom-call(f32[3,512,128]{2,1,0:T(8,128)} %fld_in.1, f32[3,512,128]{2,1,0:T(8,128)} %adj_in.1, f32[3,512,128]{2,1,0:T(8,128)} %vel_in.1, f32[512,128]{1,0:T(8,128)} %broadcast_multiply_fusion.mass_in, f32[16,8,128]{2,1,0:T(8,128)} %constant.20.clone.tab_ref, ...), custom_call_target="tpu_custom_call" | custom-call | tf_op jit(solution)/shard_map/pallas_call | solution.py:344
  57.3 0.0 copy-start
  57.3 2.1 %copy.12 = f32[3,512,128]{2,1,0:T(8,128)} copy(f32[3,512,128]{2,1,0:T(8,128)} %get-tuple-element.6) | data formatting | bytes 1572864
  59.4 0.0 copy-done
  59.4 0.9 %copy.13 = f32[3,512,128]{2,1,0:T(8,128)} copy(f32[3,512,128]{2,1,0:T(8,128)S(1)} %copy-done) | data formatting | bytes 1572864
Async XLA Ops:
  0.6 0.7 %copy-start.1 = (f32[8]{0:T(128)S(1)}, f32[8]{0:T(128)}, u32[]{:S(2)}) copy-start(f32[8]{0:T(128)} %constant.19.clone) | copy-start | bytes 100
  57.3 2.1 %copy-start = (f32[3,512,128]{2,1,0:T(8,128)S(1)}, f32[3,512,128]{2,1,0:T(8,128)}, u32[]{:S(2)}) copy-start(f32[3,512,128]{2,1,0:T(8,128)} %get-tuple-element.7) | copy-start | bytes 2359300

commit v5 on v4

--- a/solution.py
+++ b/solution.py
@@ -212,51 +212,56 @@
         sort_in(vel_in.at[f], vel_ref.at[f])
     sort_in(mass_in, mass_ref)
 
-    def plan(u):
-        face_j = lambda side: xs.at[u, :, side]
-        face_i = lambda side: xs.at[u, side]
+    groups = ((0, 1), (1, 4), (4, 7), (7, 10), (10, 13))
+
+    def plan(g):
+        lo, hi = groups[g]
+        n = hi - lo
         sends = [
-            (sj.at[u, 1], rj.at[u, 0], right, has_right),
-            (sj.at[u, 0], rj.at[u, 1], left, has_left),
-            (si.at[u, 1], ri.at[u, 0], up, has_up),
-            (si.at[u, 0], ri.at[u, 1], down, has_down),
-            (sd.at[u, 0], rd.at[u, 0], up_right, has_up & has_right),
-            (sd.at[u, 1], rd.at[u, 1], up_left, has_up & has_left),
-            (sd.at[u, 2], rd.at[u, 2], down_right, has_down & has_right),
-            (sd.at[u, 3], rd.at[u, 3], down_left, has_down & has_left),
+            (sj.at[g, 1, 0:n], rj.at[g, 0, 0:n], right, has_right),
+            (sj.at[g, 0, 0:n], rj.at[g, 1, 0:n], left, has_left),
+            (si.at[g, 1, 0:n], ri.at[g, 0, 0:n], up, has_up),
+            (si.at[g, 0, 0:n], ri.at[g, 1, 0:n], down, has_down),
+            (sd.at[g, 0, 0:n], rd.at[g, 0, 0:n], up_right, has_up & has_right),
+            (sd.at[g, 1, 0:n], rd.at[g, 1, 0:n], up_left, has_up & has_left),
+            (sd.at[g, 2, 0:n], rd.at[g, 2, 0:n], down_right, has_down & has_right),
+            (sd.at[g, 3, 0:n], rd.at[g, 3, 0:n], down_left, has_down & has_left),
         ]
         copies = [
             pltpu.make_async_remote_copy(
-                s, d, ssem.at[u, k], rsem.at[u, k], device_id=(t,), device_id_type=pl.DeviceIdType.MESH
+                s, d, ssem.at[g, k], rsem.at[g, k], device_id=(t,), device_id_type=pl.DeviceIdType.MESH
             )
             for k, (s, d, t, _) in enumerate(sends)
         ]
         recv_has = [has_left, has_right, has_down, has_up,
                     has_down & has_left, has_down & has_right, has_up & has_left, has_up & has_right]
         targets = [
-            face_j(0), face_j(7), face_i(0), face_i(7),
-            xs.at[u, 0, 0], xs.at[u, 0, 7], xs.at[u, 7, 0], xs.at[u, 7, 7],
+            xs.at[lo:hi, :, 0], xs.at[lo:hi, :, 7], xs.at[lo:hi, 0], xs.at[lo:hi, 7],
+            xs.at[lo:hi, 0, 0], xs.at[lo:hi, 0, 7], xs.at[lo:hi, 7, 0], xs.at[lo:hi, 7, 7],
         ]
         return sends, copies, recv_has, targets
 
-    def start_unit(u):
-        xs[u] = z_assemble(xs[u])
-        sj[u, 0] = xs[u, :, 0]
-        sj[u, 1] = xs[u, :, 7]
-        si[u, 0] = xs[u, 0]
-        si[u, 1] = xs[u, 7]
-        sd[u, 0] = xs[u, 7, 7]
-        sd[u, 1] = xs[u, 7, 0]
-        sd[u, 2] = xs[u, 0, 7]
-        sd[u, 3] = xs[u, 0, 0]
-        sends, copies, _, _ = plan(u)
+    def start_group(g):
+        lo, hi = groups[g]
+        n = hi - lo
+        for u in range(lo, hi):
+            xs[u] = z_assemble(xs[u])
+        sj[g, 0, 0:n] = xs[lo:hi, :, 0]
+        sj[g, 1, 0:n] = xs[lo:hi, :, 7]
+        si[g, 0, 0:n] = xs[lo:hi, 0]
+        si[g, 1, 0:n] = xs[lo:hi, 7]
+        sd[g, 0, 0:n] = xs[lo:hi, 7, 7]
+        sd[g, 1, 0:n] = xs[lo:hi, 7, 0]
+        sd[g, 2, 0:n] = xs[lo:hi, 0, 7]
+        sd[g, 3, 0:n] = xs[lo:hi, 0, 0]
+        sends, copies, _, _ = plan(g)
         for (_, _, _, has), c in zip(sends, copies):
             @pl.when(has)
             def _():
                 c.start()
 
-    def finish_unit(u):
-        sends, copies, recv_has, targets = plan(u)
+    def finish_group(g):
+        sends, copies, recv_has, targets = plan(g)
         for (_, _, _, has), c in zip(sends, copies):
             @pl.when(has)
             def _():
@@ -270,46 +275,34 @@
     def flow():
         return (vel_ref[0], vel_ref[1], vel_ref[2])
 
-    def forward_first(f):
+    xs[0] = mass_ref[...]
+    start_group(0)
+    xs[1] = forward_terms(fld_ref[0], flow(), mass_ref[...], kap_ref[0], tab_ref)
+    finish_group(0)
+    ms_ref[...] = xs[0]
+    for f in range(3):
+        xs[7 + f] = adj_ref[f] / ms_ref[...]
+    start_group(3)
+    for f in range(1, 3):
         xs[1 + f] = forward_terms(fld_ref[f], flow(), mass_ref[...], kap_ref[f], tab_ref)
-        start_unit(1 + f)
-
-    def forward_second(f):
-        finish_unit(1 + f)
+    start_group(1)
+    finish_group(3)
+    for f in range(3):
+        a1 = adj_ref[f] + time_step * adjoint_terms(xs[7 + f], flow(), mass_ref[...], kap_ref[f], tab_ref)
+        a1_ref[f] = a1
+        xs[10 + f] = a1 / ms_ref[...]
+    start_group(4)
+    finish_group(1)
+    for f in range(3):
         f1 = fld_ref[f] + time_step * xs[1 + f] / ms_ref[...]
         f1_ref[f] = f1
         xs[4 + f] = forward_terms(f1, flow(), mass_ref[...], kap_ref[f], tab_ref)
-        start_unit(4 + f)
-
-    def adjoint_second(f):
-        finish_unit(7 + f)
-        a1 = adj_ref[f] + time_step * adjoint_terms(xs[7 + f], flow(), mass_ref[...], kap_ref[f], tab_ref)
-        a1_ref[f] = a1
-        xs[10 + f] = a1 / ms_ref[...]
-        start_unit(10 + f)
-
-    def adjoint_third(f):
-        finish_unit(10 + f)
+    start_group(2)
+    finish_group(4)
+    for f in range(3):
         out_a_ref[f] = a1_ref[f] + time_step * adjoint_terms(xs[10 + f], flow(), mass_ref[...], kap_ref[f], tab_ref)
-
-    xs[0] = mass_ref[...]
-    start_unit(0)
-    forward_first(0)
-    forward_first(1)
-    finish_unit(0)
-    ms_ref[...] = xs[0]
-    for f in range(3):
-        xs[7 + f] = adj_ref[f] / ms_ref[...]
-        start_unit(7 + f)
-    forward_first(2)
-    for f in range(3):
-        forward_second(f)
-    for f in range(3):
-        adjoint_second(f)
-    for f in range(3):
-        adjoint_third(f)
-    for f in range(3):
-        finish_unit(4 + f)
+    finish_group(2)
+    for f in range(3):
         out_f_ref[f] = f1_ref[f] + time_step * xs[4 + f] / ms_ref[...]
 
     for f in range(3):
@@ -335,11 +328,12 @@
         pltpu.VMEM((3,) + cube, f32),
         pltpu.VMEM((units,) + cube, f32),
     ]
+    groups = 5
     for _ in range(4):
-        scratch.append(pltpu.VMEM((units, 2, 8, 8, 128), f32))
+        scratch.append(pltpu.VMEM((groups, 2, 3, 8, 8, 128), f32))
     for _ in range(2):
-        scratch.append(pltpu.VMEM((units, 4, 8, 128), f32))
-    scratch += [pltpu.SemaphoreType.DMA((units, 8)), pltpu.SemaphoreType.DMA((units, 8))]
+        scratch.append(pltpu.VMEM((groups, 4, 3, 8, 128), f32))
+    scratch += [pltpu.SemaphoreType.DMA((groups, 8)), pltpu.SemaphoreType.DMA((groups, 8))]
     shape = fields.shape
     return pl.pallas_call(
         functools.partial(kernel, ndev, cols),

time: 60.5 us -> 59.6 us (0.985)
  Pallas kernels: 53.2 us -> 52.4 us
    pallas_call x1, Pallas kernels: 53.2 us -> 52.4 us  [fused(): pl.pallas_call(functools.partial(kernel, ndev, cols), out_shape=(jax.Shap...]
where the time goes in v5:
time: 59.6 us; the launch traced here: 59.5 us
  Pallas kernels  52.4 us (88%)
  other arithmetic  3.29 us (6%)
  local copies, waits for them, and re-layouts  3.12 us (5%)
  between operations  0.66 us (1%)
    pallas_call x1, Pallas kernels, fused(): pl.pallas_call(functools.partial(kernel, ndev, cols), out_shape=(jax.Shap...  52.4 us
    unnamed x6, local copies, waits for them, and re-layouts  3.03 us
    mul x1, other arithmetic, shards(): mass_cube = mass_weights * weight_cube  1.79 us

profile of v5, /device:TPU:63, one launch (start us, length us, event | category | flops | bytes accessed | tf_op | source)
XLA Modules:
  0.0 59.5 jit_solution(6018192895116220879)
XLA Ops:
  0.6 0.0 copy-start.1
  0.6 0.7 %and_select_fusion = s32[128]{0:T(128)S(1)} fusion(s32[128]{0:T(128)} %param.13), kind=kLoop, calls=%fused_computation.9 | loop fusion | flops 1408 | bytes 1024 | tf_op jit(solution)/shard_map/jit(remainder)/select_n | solution.py:354
  1.3 0.0 copy-done.1
  1.3 0.1 broadcast_multiply_fusion.2
  1.4 0.1 broadcast_multiply_fusion.1
  1.5 0.1 mul.52
  1.6 0.7 %fusion.1 = (bf16[128,128]{1,0:T(8,128)(2,1)}, bf16[128,128]{1,0:T(8,128)(2,1)}) fusion(s32[128]{0:T(128)S(1)} %and_select_fusion), kind=kLoop, calls=%fused_computation.4 | loop fusion | flops 65536 | bytes 66048 | tf_op jit(solution)/shard_map/convert_element_type | solution.py:357
  2.2 1.8 %broadcast_multiply_fusion.mass_in = f32[512,128]{1,0:T(8,128)} fusion(f32[512,128]{1,0:T(8,128)} %param.11, f32[512]{0:T(512)S(1)} %mul.52), kind=kLoop, calls=%fused_computation | loop fusion | flops 65536 | bytes 526336 | tf_op jit(solution)/shard_map/mul | solution.py:360
  4.0 52.4 %shard_map.95 = (f32[3,512,128]{2,1,0:T(8,128)}, f32[3,512,128]{2,1,0:T(8,128)}) custom-call(f32[3,512,128]{2,1,0:T(8,128)} %fld_in.1, f32[3,512,128]{2,1,0:T(8,128)} %adj_in.1, f32[3,512,128]{2,1,0:T(8,128)} %vel_in.1, f32[512,128]{1,0:T(8,128)} %broadcast_multiply_fusion.mass_in, f32[16,8,128]{2,1,0:T(8,128)} %constant.20.clone.tab_ref, ...), custom_call_target="tpu_custom_call" | custom-call | tf_op jit(solution)/shard_map/pallas_call | solution.py:338
  56.4 0.0 copy-start
  56.4 2.1 %copy.12 = f32[3,512,128]{2,1,0:T(8,128)} copy(f32[3,512,128]{2,1,0:T(8,128)} %get-tuple-element.6) | data formatting | bytes 1572864
  58.6 0.0 copy-done
  58.6 0.9 %copy.13 = f32[3,512,128]{2,1,0:T(8,128)} copy(f32[3,512,128]{2,1,0:T(8,128)S(1)} %copy-done) | data formatting | bytes 1572864
Async XLA Ops:
  0.6 0.7 %copy-start.1 = (f32[8]{0:T(128)S(1)}, f32[8]{0:T(128)}, u32[]{:S(2)}) copy-start(f32[8]{0:T(128)} %constant.19.clone) | copy-start | bytes 100
  56.4 2.1 %copy-start = (f32[3,512,128]{2,1,0:T(8,128)S(1)}, f32[3,512,128]{2,1,0:T(8,128)}, u32[]{:S(2)}) copy-start(f32[3,512,128]{2,1,0:T(8,128)} %get-tuple-element.7) | copy-start | bytes 2359300

commit v6 on v5

--- a/solution.py
+++ b/solution.py
@@ -212,7 +212,7 @@
         sort_in(vel_in.at[f], vel_ref.at[f])
     sort_in(mass_in, mass_ref)
 
-    groups = ((0, 1), (1, 4), (4, 7), (7, 10), (10, 13))
+    groups = ((0, 4), (4, 7), (7, 10), (10, 13))
 
     def plan(g):
         lo, hi = groups[g]
@@ -276,34 +276,32 @@
         return (vel_ref[0], vel_ref[1], vel_ref[2])
 
     xs[0] = mass_ref[...]
+    for f in range(3):
+        xs[1 + f] = adj_ref[f]
     start_group(0)
-    xs[1] = forward_terms(fld_ref[0], flow(), mass_ref[...], kap_ref[0], tab_ref)
+    for f in range(3):
+        xs[4 + f] = forward_terms(fld_ref[f], flow(), mass_ref[...], kap_ref[f], tab_ref)
+    start_group(1)
     finish_group(0)
     ms_ref[...] = xs[0]
     for f in range(3):
-        xs[7 + f] = adj_ref[f] / ms_ref[...]
+        gathered = xs[1 + f] / ms_ref[...]
+        a1 = adj_ref[f] + time_step * adjoint_terms(gathered, flow(), mass_ref[...], kap_ref[f], tab_ref)
+        a1_ref[f] = a1
+        xs[7 + f] = a1 / ms_ref[...]
+    start_group(2)
+    finish_group(1)
+    for f in range(3):
+        f1 = fld_ref[f] + time_step * xs[4 + f] / ms_ref[...]
+        f1_ref[f] = f1
+        xs[10 + f] = forward_terms(f1, flow(), mass_ref[...], kap_ref[f], tab_ref)
     start_group(3)
-    for f in range(1, 3):
-        xs[1 + f] = forward_terms(fld_ref[f], flow(), mass_ref[...], kap_ref[f], tab_ref)
-    start_group(1)
+    finish_group(2)
+    for f in range(3):
+        out_a_ref[f] = a1_ref[f] + time_step * adjoint_terms(xs[7 + f], flow(), mass_ref[...], kap_ref[f], tab_ref)
     finish_group(3)
     for f in range(3):
-        a1 = adj_ref[f] + time_step * adjoint_terms(xs[7 + f], flow(), mass_ref[...], kap_ref[f], tab_ref)
-        a1_ref[f] = a1
-        xs[10 + f] = a1 / ms_ref[...]
-    start_group(4)
-    finish_group(1)
-    for f in range(3):
-        f1 = fld_ref[f] + time_step * xs[1 + f] / ms_ref[...]
-        f1_ref[f] = f1
-        xs[4 + f] = forward_terms(f1, flow(), mass_ref[...], kap_ref[f], tab_ref)
-    start_group(2)
-    finish_group(4)
-    for f in range(3):
-        out_a_ref[f] = a1_ref[f] + time_step * adjoint_terms(xs[10 + f], flow(), mass_ref[...], kap_ref[f], tab_ref)
-    finish_group(2)
-    for f in range(3):
-        out_f_ref[f] = f1_ref[f] + time_step * xs[4 + f] / ms_ref[...]
+        out_f_ref[f] = f1_ref[f] + time_step * xs[10 + f] / ms_ref[...]
 
     for f in range(3):
         out_f_in[f] = permute(out_f_ref[f].reshape(512, 128), pout_ref[...])
@@ -328,11 +326,11 @@
         pltpu.VMEM((3,) + cube, f32),
         pltpu.VMEM((units,) + cube, f32),
     ]
-    groups = 5
+    groups = 4
     for _ in range(4):
-        scratch.append(pltpu.VMEM((groups, 2, 3, 8, 8, 128), f32))
+        scratch.append(pltpu.VMEM((groups, 2, 4, 8, 8, 128), f32))
     for _ in range(2):
-        scratch.append(pltpu.VMEM((groups, 4, 3, 8, 128), f32))
+        scratch.append(pltpu.VMEM((groups, 4, 4, 8, 128), f32))
     scratch += [pltpu.SemaphoreType.DMA((groups, 8)), pltpu.SemaphoreType.DMA((groups, 8))]
     shape = fields.shape
     return pl.pallas_call(

time: 59.6 us -> 54.8 us (0.919)
  Pallas kernels: 52.4 us -> 47.5 us
    pallas_call x1, Pallas kernels: 52.4 us -> 47.5 us  [fused(): pl.pallas_call(functools.partial(kernel, ndev, cols), out_shape=(jax.Shap...]
where the time goes in v6:
time: 54.8 us; the launch traced here: 54.6 us
  Pallas kernels  47.5 us (87%)
  other arithmetic  3.29 us (6%)
  local copies, waits for them, and re-layouts  3.12 us (6%)
  between operations  0.66 us (1%)
    pallas_call x1, Pallas kernels, fused(): pl.pallas_call(functools.partial(kernel, ndev, cols), out_shape=(jax.Shap...  47.5 us
    unnamed x6, local copies, waits for them, and re-layouts  3.03 us
    mul x1, other arithmetic, shards(): mass_cube = mass_weights * weight_cube  1.79 us

profile of v6, /device:TPU:63, one launch (start us, length us, event | category | flops | bytes accessed | tf_op | source)
XLA Modules:
  0.0 54.6 jit_solution(3814022442803982010)
XLA Ops:
  0.6 0.0 copy-start.1
  0.6 0.7 %and_select_fusion = s32[128]{0:T(128)S(1)} fusion(s32[128]{0:T(128)} %param.13), kind=kLoop, calls=%fused_computation.9 | loop fusion | flops 1408 | bytes 1024 | tf_op jit(solution)/shard_map/jit(remainder)/select_n | solution.py:352
  1.3 0.0 copy-done.1
  1.3 0.1 broadcast_multiply_fusion.2
  1.4 0.1 broadcast_multiply_fusion.1
  1.5 0.1 mul.52
  1.6 0.7 %fusion.1 = (bf16[128,128]{1,0:T(8,128)(2,1)}, bf16[128,128]{1,0:T(8,128)(2,1)}) fusion(s32[128]{0:T(128)S(1)} %and_select_fusion), kind=kLoop, calls=%fused_computation.4 | loop fusion | flops 65536 | bytes 66048 | tf_op jit(solution)/shard_map/convert_element_type | solution.py:355
  2.2 1.8 %broadcast_multiply_fusion.mass_in = f32[512,128]{1,0:T(8,128)} fusion(f32[512,128]{1,0:T(8,128)} %param.11, f32[512]{0:T(512)S(1)} %mul.52), kind=kLoop, calls=%fused_computation | loop fusion | flops 65536 | bytes 526336 | tf_op jit(solution)/shard_map/mul | solution.py:358
  4.0 47.5 %shard_map.95 = (f32[3,512,128]{2,1,0:T(8,128)}, f32[3,512,128]{2,1,0:T(8,128)}) custom-call(f32[3,512,128]{2,1,0:T(8,128)} %fld_in.1, f32[3,512,128]{2,1,0:T(8,128)} %adj_in.1, f32[3,512,128]{2,1,0:T(8,128)} %vel_in.1, f32[512,128]{1,0:T(8,128)} %broadcast_multiply_fusion.mass_in, f32[16,8,128]{2,1,0:T(8,128)} %constant.20.clone.tab_ref, ...), custom_call_target="tpu_custom_call" | custom-call | tf_op jit(solution)/shard_map/pallas_call | solution.py:336
  51.6 0.0 copy-start
  51.6 2.1 %copy.12 = f32[3,512,128]{2,1,0:T(8,128)} copy(f32[3,512,128]{2,1,0:T(8,128)} %get-tuple-element.6) | data formatting | bytes 1572864
  53.7 0.0 copy-done
  53.7 0.9 %copy.13 = f32[3,512,128]{2,1,0:T(8,128)} copy(f32[3,512,128]{2,1,0:T(8,128)S(1)} %copy-done) | data formatting | bytes 1572864
Async XLA Ops:
  0.6 0.7 %copy-start.1 = (f32[8]{0:T(128)S(1)}, f32[8]{0:T(128)}, u32[]{:S(2)}) copy-start(f32[8]{0:T(128)} %constant.19.clone) | copy-start | bytes 100
  51.6 2.1 %copy-start = (f32[3,512,128]{2,1,0:T(8,128)S(1)}, f32[3,512,128]{2,1,0:T(8,128)}, u32[]{:S(2)}) copy-start(f32[3,512,128]{2,1,0:T(8,128)} %get-tuple-element.7) | copy-start | bytes 2359300

commit v7 on v6

--- a/solution.py
+++ b/solution.py
@@ -68,7 +68,9 @@
         for p in range(8):
             fwd[s, p, :] = DM[p, (p - s) % 8]
             bwd[s, p, :] = DM[(p - s) % 8, p]
-    return np.concatenate([fwd, bwd], axis=0)
+    cube = (WEIGHTS[:, None, None] * WEIGHTS[None, :, None]) * WEIGHTS[None, None, :]
+    wrows = np.broadcast_to(cube.reshape(64, 8, 1), (64, 8, 128)).astype(np.float32)
+    return np.concatenate([fwd, bwd, wrows], axis=0)
 
 
 def along_major(v, axis, transpose):
@@ -136,16 +138,19 @@
     return v + jnp.where((sub == 7) & (lane < 127), above, zero)
 
 
-def permute(x, pm):
+def permute(x, pm, transpose):
     bf = jnp.bfloat16
     f32 = jnp.float32
+    dims = (((1,), (1,) if transpose else (0,)), ((), ()))
+
+    def dot(a):
+        return lax.dot_general(a, pm, dims, preferred_element_type=f32)
+
     x1 = x.astype(bf)
     r1 = x - x1.astype(f32)
     x2 = r1.astype(bf)
     x3 = (r1 - x2.astype(f32)).astype(bf)
-    y = jnp.dot(x1, pm, preferred_element_type=f32)
-    y = y + jnp.dot(x2, pm, preferred_element_type=f32)
-    return y + jnp.dot(x3, pm, preferred_element_type=f32)
+    return dot(x1) + dot(x2) + dot(x3)
 
 
 def kernel(
@@ -156,8 +161,7 @@
     vel_in,
     mass_in,
     tab_ref,
-    pin_ref,
-    pout_ref,
+    num_ref,
     kap_ref,
     out_f_in,
     out_a_in,
@@ -203,14 +207,19 @@
         pl.semaphore_signal(barrier, inc=1, device_id=(nb,), device_id_type=pl.DeviceIdType.MESH)
     pl.semaphore_wait(barrier, 8)
 
+    count = num_ref.shape[1]
+    height = lax.rem(num_ref[...], count)
+    p_out = (lax.broadcasted_iota(jnp.int32, (count, count), 0) == height).astype(jnp.bfloat16)
+
     def sort_in(src_ref, dst_ref):
-        dst_ref[...] = permute(src_ref[...], pin_ref[...]).reshape(dst_ref.shape)
+        dst_ref[...] = permute(src_ref[...], p_out, True).reshape(dst_ref.shape)
 
     for f in range(3):
         sort_in(fld_in.at[f], fld_ref.at[f])
         sort_in(adj_in.at[f], adj_ref.at[f])
         sort_in(vel_in.at[f], vel_ref.at[f])
     sort_in(mass_in, mass_ref)
+    mass_ref[...] = mass_ref[...] * tab_ref[16:80].reshape(mass_ref.shape)
 
     groups = ((0, 4), (4, 7), (7, 10), (10, 13))
 
@@ -304,11 +313,11 @@
         out_f_ref[f] = f1_ref[f] + time_step * xs[10 + f] / ms_ref[...]
 
     for f in range(3):
-        out_f_in[f] = permute(out_f_ref[f].reshape(512, 128), pout_ref[...])
-        out_a_in[f] = permute(out_a_ref[f].reshape(512, 128), pout_ref[...])
-
-
-def fused(fields, adjoint, flow, mass, table, p_in, p_out, kappa, ndev, cols):
+        out_f_in[f] = permute(out_f_ref[f].reshape(512, 128), p_out, False)
+        out_a_in[f] = permute(out_a_ref[f].reshape(512, 128), p_out, False)
+
+
+def fused(fields, adjoint, flow, mass, table, numbering, kappa, ndev, cols):
     cube = (8, 8, 8, 128)
     f32 = jnp.float32
     units = 13
@@ -336,28 +345,23 @@
     return pl.pallas_call(
         functools.partial(kernel, ndev, cols),
         out_shape=(jax.ShapeDtypeStruct(shape, f32), jax.ShapeDtypeStruct(shape, f32)),
-        in_specs=[vmem, vmem, vmem, vmem, vmem, vmem, vmem, smem],
+        in_specs=[vmem, vmem, vmem, vmem, vmem, vmem, smem],
         out_specs=(vmem, vmem),
         scratch_shapes=scratch,
         compiler_params=pltpu.CompilerParams(
             collective_id=0, has_side_effects=True, vmem_limit_bytes=60 * 1024 * 1024
         ),
-    )(fields, adjoint, flow, mass, table, p_in, p_out, kappa)
+    )(fields, adjoint, flow, mass, table, numbering, kappa)
 
 
 def shards(moment_fields, adjoint_fields, velocity, mass_weights, diffusivity, numbering):
-    height_count = numbering.shape[0]
     ndev = lax.axis_size("elem")
     cols = ndev // DA
-    height = numbering % height_count
-    slot_index = lax.iota(jnp.int32, height_count)
-    p_in = (height[:, None] == slot_index[None, :]).astype(jnp.bfloat16)
-    p_out = (slot_index[:, None] == height[None, :]).astype(jnp.bfloat16)
-    weights = jnp.asarray(WEIGHTS)
-    weight_cube = (weights[:, None, None] * weights[None, :, None] * weights[None, None, :]).reshape(512, 1)
-    mass_cube = mass_weights * weight_cube
     table = jnp.asarray(shift_tables())
-    return fused(moment_fields, adjoint_fields, velocity, mass_cube, table, p_in, p_out, diffusivity, ndev, cols)
+    return fused(
+        moment_fields, adjoint_fields, velocity, mass_weights, table,
+        numbering.reshape(1, -1), diffusivity, ndev, cols,
+    )
 
 
 def solution(mesh):

time: 54.8 us -> 51.5 us (0.940)
  other arithmetic: 3.29 us -> 0 us
    mul x3 -> x0, other arithmetic: 1.93 us -> none  [the longest x1 1.79 us: shards(): mass_cube = mass_weights * weight_cube]
    convert_element_type x1 -> x0, other arithmetic: 0.69 us -> none  [shards(): p_out = (slot_index[:, None] == height[None, :]).astype(jnp.bfloat16)]
    select_n x1 -> x0, other arithmetic: 0.67 us -> none  [shards(): height = numbering % height_count]
    unnamed x6 -> x4, local copies, waits for them, and re-layouts: 3.03 us -> 3.02 us
where the time goes in v7:
time: 51.5 us; the launch traced here: 51.3 us
  Pallas kernels  47.7 us (93%)
  local copies, waits for them, and re-layouts  3.02 us (6%)
  between operations  0.65 us (1%)
    pallas_call x1, Pallas kernels, fused(): pl.pallas_call(functools.partial(kernel, ndev, cols), out_shape=(jax.Shap...  47.7 us
    unnamed x4, local copies, waits for them, and re-layouts  3.02 us

profile of v7, /device:TPU:63, one launch (start us, length us, event | category | flops | bytes accessed | tf_op | source)
XLA Modules:
  0.0 51.3 jit_solution(15397907043636793115)
XLA Ops:
  0.6 47.7 %shard_map.86 = (f32[3,512,128]{2,1,0:T(8,128)}, f32[3,512,128]{2,1,0:T(8,128)}) custom-call(f32[3,512,128]{2,1,0:T(8,128)} %fld_in.1, f32[3,512,128]{2,1,0:T(8,128)} %adj_in.1, f32[3,512,128]{2,1,0:T(8,128)} %vel_in.1, f32[512,128]{1,0:T(8,128)} %mass_in.1, f32[80,8,128]{2,1,0:T(8,128)} %constant.2.clone.tab_ref, s32[1,128]{1,0:T(1,128)} %bitcast.1, f32[3]{0:T(128)} %kap_ref.1), custom_call_target="tpu_custom_call" | custom-call | tf_op jit(solution)/shard_map/pallas_call | solution.py:345
  48.3 0.0 copy-start
  48.3 2.1 %copy.11 = f32[3,512,128]{2,1,0:T(8,128)} copy(f32[3,512,128]{2,1,0:T(8,128)} %get-tuple-element.4) | data formatting | bytes 1572864
  50.4 0.0 copy-done
  50.4 0.9 %copy.12 = f32[3,512,128]{2,1,0:T(8,128)} copy(f32[3,512,128]{2,1,0:T(8,128)S(1)} %copy-done) | data formatting | bytes 1572864
Async XLA Ops:
  48.3 2.1 %copy-start = (f32[3,512,128]{2,1,0:T(8,128)S(1)}, f32[3,512,128]{2,1,0:T(8,128)}, u32[]{:S(2)}) copy-start(f32[3,512,128]{2,1,0:T(8,128)} %get-tuple-element.5) | copy-start | bytes 2359300

commit v8 on v7

--- a/solution.py
+++ b/solution.py
@@ -205,7 +205,6 @@
     barrier = pltpu.get_barrier_semaphore()
     for nb in (left, right, up, down, up_right, up_left, down_right, down_left):
         pl.semaphore_signal(barrier, inc=1, device_id=(nb,), device_id_type=pl.DeviceIdType.MESH)
-    pl.semaphore_wait(barrier, 8)
 
     count = num_ref.shape[1]
     height = lax.rem(num_ref[...], count)
@@ -215,9 +214,7 @@
         dst_ref[...] = permute(src_ref[...], p_out, True).reshape(dst_ref.shape)
 
     for f in range(3):
-        sort_in(fld_in.at[f], fld_ref.at[f])
         sort_in(adj_in.at[f], adj_ref.at[f])
-        sort_in(vel_in.at[f], vel_ref.at[f])
     sort_in(mass_in, mass_ref)
     mass_ref[...] = mass_ref[...] * tab_ref[16:80].reshape(mass_ref.shape)
 
@@ -251,6 +248,10 @@
         return sends, copies, recv_has, targets
 
     def start_group(g):
+        prep_group(g)
+        launch_group(g)
+
+    def prep_group(g):
         lo, hi = groups[g]
         n = hi - lo
         for u in range(lo, hi):
@@ -263,6 +264,8 @@
         sd[g, 1, 0:n] = xs[lo:hi, 7, 0]
         sd[g, 2, 0:n] = xs[lo:hi, 0, 7]
         sd[g, 3, 0:n] = xs[lo:hi, 0, 0]
+
+    def launch_group(g):
         sends, copies, _, _ = plan(g)
         for (_, _, _, has), c in zip(sends, copies):
             @pl.when(has)
@@ -287,7 +290,12 @@
     xs[0] = mass_ref[...]
     for f in range(3):
         xs[1 + f] = adj_ref[f]
-    start_group(0)
+    prep_group(0)
+    pl.semaphore_wait(barrier, 8)
+    launch_group(0)
+    for f in range(3):
+        sort_in(fld_in.at[f], fld_ref.at[f])
+        sort_in(vel_in.at[f], vel_ref.at[f])
     for f in range(3):
         xs[4 + f] = forward_terms(fld_ref[f], flow(), mass_ref[...], kap_ref[f], tab_ref)
     start_group(1)
@@ -308,13 +316,12 @@
     finish_group(2)
     for f in range(3):
         out_a_ref[f] = a1_ref[f] + time_step * adjoint_terms(xs[7 + f], flow(), mass_ref[...], kap_ref[f], tab_ref)
+    for f in range(3):
+        out_a_in[f] = permute(out_a_ref[f].reshape(512, 128), p_out, False)
     finish_group(3)
     for f in range(3):
         out_f_ref[f] = f1_ref[f] + time_step * xs[10 + f] / ms_ref[...]
-
-    for f in range(3):
         out_f_in[f] = permute(out_f_ref[f].reshape(512, 128), p_out, False)
-        out_a_in[f] = permute(out_a_ref[f].reshape(512, 128), p_out, False)
 
 
 def fused(fields, adjoint, flow, mass, table, numbering, kappa, ndev, cols):

time: 51.5 us -> 49.6 us (0.963)
  Pallas kernels: 47.7 us -> 45.8 us
    pallas_call x1, Pallas kernels: 47.7 us -> 45.8 us  [fused(): pl.pallas_call(functools.partial(kernel, ndev, cols), out_shape=(jax.Shap...]
where the time goes in v8:
time: 49.6 us; the launch traced here: 49.4 us
  Pallas kernels  45.8 us (92%)
  local copies, waits for them, and re-layouts  3.02 us (6%)
  between operations  0.65 us (1%)
    pallas_call x1, Pallas kernels, fused(): pl.pallas_call(functools.partial(kernel, ndev, cols), out_shape=(jax.Shap...  45.8 us
    unnamed x4, local copies, waits for them, and re-layouts  3.02 us

profile of v8, /device:TPU:63, one launch (start us, length us, event | category | flops | bytes accessed | tf_op | source)
XLA Modules:
  0.0 49.4 jit_solution(8955557298767270115)
XLA Ops:
  0.6 45.8 %shard_map.86 = (f32[3,512,128]{2,1,0:T(8,128)}, f32[3,512,128]{2,1,0:T(8,128)}) custom-call(f32[3,512,128]{2,1,0:T(8,128)} %fld_in.1, f32[3,512,128]{2,1,0:T(8,128)} %adj_in.1, f32[3,512,128]{2,1,0:T(8,128)} %vel_in.1, f32[512,128]{1,0:T(8,128)} %mass_in.1, f32[80,8,128]{2,1,0:T(8,128)} %constant.2.clone.tab_ref, s32[1,128]{1,0:T(1,128)} %bitcast.1, f32[3]{0:T(128)} %kap_ref.1), custom_call_target="tpu_custom_call" | custom-call | tf_op jit(solution)/shard_map/pallas_call | solution.py:352
  46.4 0.0 copy-start
  46.4 2.1 %copy.11 = f32[3,512,128]{2,1,0:T(8,128)} copy(f32[3,512,128]{2,1,0:T(8,128)} %get-tuple-element.4) | data formatting | bytes 1572864
  48.6 0.0 copy-done
  48.6 0.9 %copy.12 = f32[3,512,128]{2,1,0:T(8,128)} copy(f32[3,512,128]{2,1,0:T(8,128)S(1)} %copy-done) | data formatting | bytes 1572864
Async XLA Ops:
  46.4 2.1 %copy-start = (f32[3,512,128]{2,1,0:T(8,128)S(1)}, f32[3,512,128]{2,1,0:T(8,128)}, u32[]{:S(2)}) copy-start(f32[3,512,128]{2,1,0:T(8,128)} %get-tuple-element.5) | copy-start | bytes 2359300

commit v9 on v8

--- a/solution.py
+++ b/solution.py
@@ -218,7 +218,7 @@
     sort_in(mass_in, mass_ref)
     mass_ref[...] = mass_ref[...] * tab_ref[16:80].reshape(mass_ref.shape)
 
-    groups = ((0, 4), (4, 7), (7, 10), (10, 13))
+    groups = ((0, 4),) + tuple((u, u + 1) for u in range(4, 13))
 
     def plan(g):
         lo, hi = groups[g]
@@ -298,7 +298,7 @@
         sort_in(vel_in.at[f], vel_ref.at[f])
     for f in range(3):
         xs[4 + f] = forward_terms(fld_ref[f], flow(), mass_ref[...], kap_ref[f], tab_ref)
-    start_group(1)
+        start_group(1 + f)
     finish_group(0)
     ms_ref[...] = xs[0]
     for f in range(3):
@@ -306,20 +306,19 @@
         a1 = adj_ref[f] + time_step * adjoint_terms(gathered, flow(), mass_ref[...], kap_ref[f], tab_ref)
         a1_ref[f] = a1
         xs[7 + f] = a1 / ms_ref[...]
-    start_group(2)
-    finish_group(1)
-    for f in range(3):
+        start_group(4 + f)
+    for f in range(3):
+        finish_group(1 + f)
         f1 = fld_ref[f] + time_step * xs[4 + f] / ms_ref[...]
         f1_ref[f] = f1
         xs[10 + f] = forward_terms(f1, flow(), mass_ref[...], kap_ref[f], tab_ref)
-    start_group(3)
-    finish_group(2)
-    for f in range(3):
+        start_group(7 + f)
+    for f in range(3):
+        finish_group(4 + f)
         out_a_ref[f] = a1_ref[f] + time_step * adjoint_terms(xs[7 + f], flow(), mass_ref[...], kap_ref[f], tab_ref)
-    for f in range(3):
         out_a_in[f] = permute(out_a_ref[f].reshape(512, 128), p_out, False)
-    finish_group(3)
-    for f in range(3):
+    for f in range(3):
+        finish_group(7 + f)
         out_f_ref[f] = f1_ref[f] + time_step * xs[10 + f] / ms_ref[...]
         out_f_in[f] = permute(out_f_ref[f].reshape(512, 128), p_out, False)
 
@@ -342,7 +341,7 @@
         pltpu.VMEM((3,) + cube, f32),
         pltpu.VMEM((units,) + cube, f32),
     ]
-    groups = 4
+    groups = 10
     for _ in range(4):
         scratch.append(pltpu.VMEM((groups, 2, 4, 8, 8, 128), f32))
     for _ in range(2):

time: 49.6 us -> 49.2 us (level)
  no operation moved by 1% of the time
where the time goes in v9:
time: 49.2 us; the launch traced here: 49.1 us
  Pallas kernels  45.4 us (92%)
  local copies, waits for them, and re-layouts  3.02 us (6%)
  between operations  0.65 us (1%)
    pallas_call x1, Pallas kernels, fused(): pl.pallas_call(functools.partial(kernel, ndev, cols), out_shape=(jax.Shap...  45.4 us
    unnamed x4, local copies, waits for them, and re-layouts  3.02 us

profile of v9, /device:TPU:63, one launch (start us, length us, event | category | flops | bytes accessed | tf_op | source)
XLA Modules:
  0.0 49.1 jit_solution(11383673707095138241)
XLA Ops:
  0.6 45.4 %shard_map.86 = (f32[3,512,128]{2,1,0:T(8,128)}, f32[3,512,128]{2,1,0:T(8,128)}) custom-call(f32[3,512,128]{2,1,0:T(8,128)} %fld_in.1, f32[3,512,128]{2,1,0:T(8,128)} %adj_in.1, f32[3,512,128]{2,1,0:T(8,128)} %vel_in.1, f32[512,128]{1,0:T(8,128)} %mass_in.1, f32[80,8,128]{2,1,0:T(8,128)} %constant.2.clone.tab_ref, s32[1,128]{1,0:T(1,128)} %bitcast.1, f32[3]{0:T(128)} %kap_ref.1), custom_call_target="tpu_custom_call" | custom-call | tf_op jit(solution)/shard_map/pallas_call | solution.py:351
  46.1 0.0 copy-start
  46.1 2.1 %copy.11 = f32[3,512,128]{2,1,0:T(8,128)} copy(f32[3,512,128]{2,1,0:T(8,128)} %get-tuple-element.4) | data formatting | bytes 1572864
  48.2 0.0 copy-done
  48.2 0.9 %copy.12 = f32[3,512,128]{2,1,0:T(8,128)} copy(f32[3,512,128]{2,1,0:T(8,128)S(1)} %copy-done) | data formatting | bytes 1572864
Async XLA Ops:
  46.1 2.1 %copy-start = (f32[3,512,128]{2,1,0:T(8,128)S(1)}, f32[3,512,128]{2,1,0:T(8,128)}, u32[]{:S(2)}) copy-start(f32[3,512,128]{2,1,0:T(8,128)} %get-tuple-element.5) | copy-start | bytes 2359300

commit v10 on v9

--- a/solution.py
+++ b/solution.py
@@ -316,11 +316,31 @@
     for f in range(3):
         finish_group(4 + f)
         out_a_ref[f] = a1_ref[f] + time_step * adjoint_terms(xs[7 + f], flow(), mass_ref[...], kap_ref[f], tab_ref)
-        out_a_in[f] = permute(out_a_ref[f].reshape(512, 128), p_out, False)
+        out_a_in[f] = out_a_ref[f].reshape(512, 128)
     for f in range(3):
         finish_group(7 + f)
         out_f_ref[f] = f1_ref[f] + time_step * xs[10 + f] / ms_ref[...]
-        out_f_in[f] = permute(out_f_ref[f].reshape(512, 128), p_out, False)
+        out_f_in[f] = out_f_ref[f].reshape(512, 128)
+
+
+def unsort_kernel(num_ref, f_ref, a_ref, out_f, out_a):
+    count = num_ref.shape[1]
+    height = lax.rem(num_ref[...], count)
+    p_out = (lax.broadcasted_iota(jnp.int32, (count, count), 0) == height).astype(jnp.bfloat16)
+    for f in range(f_ref.shape[0]):
+        out_f[f] = permute(f_ref[f], p_out, False)
+        out_a[f] = permute(a_ref[f], p_out, False)
+
+
+def unsort(numbering, moments, sensitivities):
+    vmem = pl.BlockSpec(memory_space=pltpu.VMEM)
+    shape = jax.ShapeDtypeStruct(moments.shape, jnp.float32)
+    return pl.pallas_call(
+        unsort_kernel,
+        out_shape=(shape, shape),
+        in_specs=[vmem, vmem, vmem],
+        out_specs=(vmem, vmem),
+    )(numbering, moments, sensitivities)
 
 
 def fused(fields, adjoint, flow, mass, table, numbering, kappa, ndev, cols):
@@ -364,10 +384,12 @@
     ndev = lax.axis_size("elem")
     cols = ndev // DA
     table = jnp.asarray(shift_tables())
-    return fused(
+    row_numbers = numbering.reshape(1, -1)
+    moments, sensitivities = fused(
         moment_fields, adjoint_fields, velocity, mass_weights, table,
-        numbering.reshape(1, -1), diffusivity, ndev, cols,
+        row_numbers, diffusivity, ndev, cols,
     )
+    return unsort(row_numbers, moments, sensitivities)
 
 
 def solution(mesh):

time: 49.2 us -> 49.5 us (level)
  Pallas kernels: 45.4 us -> 48.7 us
  local copies, waits for them, and re-layouts: 3.02 us -> 0 us
    pallas_call x0 -> x1, Pallas kernels: none -> 3.3 us  [unsort(): pl.pallas_call(unsort_kernel, out_shape=(shape, shape), in_specs=[vmem, v...]
    unnamed x4 -> x0, local copies, waits for them, and re-layouts: 3.02 us -> none
where the time goes in v10:
time: 49.5 us; the launch traced here: 49.3 us
  Pallas kernels  48.7 us (98%)
  between operations  0.64 us (1%)
    pallas_call x1, Pallas kernels, fused(): pl.pallas_call(functools.partial(kernel, ndev, cols), out_shape=(jax.Shap...  45.4 us
    pallas_call x1, Pallas kernels, unsort(): pl.pallas_call(unsort_kernel, out_shape=(shape, shape), in_specs=[vmem, v...  3.3 us

profile of v10, /device:TPU:63, one launch (start us, length us, event | category | flops | bytes accessed | tf_op | source)
XLA Modules:
  0.0 49.3 jit_solution(11213970160114386686)
XLA Ops:
  0.6 45.4 %shard_map.86 = (f32[3,512,128]{2,1,0:T(8,128)}, f32[3,512,128]{2,1,0:T(8,128)}) custom-call(f32[3,512,128]{2,1,0:T(8,128)} %fld_in.1, f32[3,512,128]{2,1,0:T(8,128)} %adj_in.1, f32[3,512,128]{2,1,0:T(8,128)} %vel_in.1, f32[512,128]{1,0:T(8,128)} %mass_in.1, f32[80,8,128]{2,1,0:T(8,128)} %constant.2.clone.tab_ref, s32[1,128]{1,0:T(1,128)} %bitcast.1, f32[3]{0:T(128)} %kap_ref.1), custom_call_target="tpu_custom_call" | custom-call | tf_op jit(solution)/shard_map/pallas_call | solution.py:371
  46.0 3.3 %shard_map.87 = (f32[3,512,128]{2,1,0:T(8,128)}, f32[3,512,128]{2,1,0:T(8,128)}) custom-call(s32[1,128]{1,0:T(1,128)} %bitcast.2, f32[3,512,128]{2,1,0:T(8,128)} %get-tuple-element.4.f_ref, f32[3,512,128]{2,1,0:T(8,128)} %get-tuple-element.5.a_ref), custom_call_target="tpu_custom_call" | custom-call | tf_op jit(solution)/shard_map/pallas_call | solution.py:338

commit v11 on v10

--- a/solution.py
+++ b/solution.py
@@ -327,19 +327,20 @@
     count = num_ref.shape[1]
     height = lax.rem(num_ref[...], count)
     p_out = (lax.broadcasted_iota(jnp.int32, (count, count), 0) == height).astype(jnp.bfloat16)
-    for f in range(f_ref.shape[0]):
-        out_f[f] = permute(f_ref[f], p_out, False)
-        out_a[f] = permute(a_ref[f], p_out, False)
+    out_f[0] = permute(f_ref[0], p_out, False)
+    out_a[0] = permute(a_ref[0], p_out, False)
 
 
 def unsort(numbering, moments, sensitivities):
-    vmem = pl.BlockSpec(memory_space=pltpu.VMEM)
+    count, nodes, width = moments.shape
+    block = pl.BlockSpec((1, nodes, width), lambda f: (f, 0, 0))
     shape = jax.ShapeDtypeStruct(moments.shape, jnp.float32)
     return pl.pallas_call(
         unsort_kernel,
+        grid=(count,),
         out_shape=(shape, shape),
-        in_specs=[vmem, vmem, vmem],
-        out_specs=(vmem, vmem),
+        in_specs=[pl.BlockSpec(numbering.shape, lambda f: (0, 0)), block, block],
+        out_specs=(block, block),
     )(numbering, moments, sensitivities)
 
 

time: 49.5 us -> 50 us (1.010)
  Pallas kernels: 48.7 us -> 49.2 us
    pallas_call x1, Pallas kernels: 3.3 us -> 3.81 us  [unsort(): pl.pallas_call(unsort_kernel, grid=(count,), out_shape=(shape, shape), in...]
where the time goes in v11:
time: 50 us; the launch traced here: 49.8 us
  Pallas kernels  49.2 us (98%)
  between operations  0.64 us (1%)
    pallas_call x1, Pallas kernels, fused(): pl.pallas_call(functools.partial(kernel, ndev, cols), out_shape=(jax.Shap...  45.4 us
    pallas_call x1, Pallas kernels, unsort(): pl.pallas_call(unsort_kernel, grid=(count,), out_shape=(shape, shape), in...  3.81 us

profile of v11, /device:TPU:63, one launch (start us, length us, event | category | flops | bytes accessed | tf_op | source)
XLA Modules:
  0.0 49.8 jit_solution(64995585141107062)
XLA Ops:
  0.6 45.4 %shard_map.86 = (f32[3,512,128]{2,1,0:T(8,128)}, f32[3,512,128]{2,1,0:T(8,128)}) custom-call(f32[3,512,128]{2,1,0:T(8,128)} %fld_in.1, f32[3,512,128]{2,1,0:T(8,128)} %adj_in.1, f32[3,512,128]{2,1,0:T(8,128)} %vel_in.1, f32[512,128]{1,0:T(8,128)} %mass_in.1, f32[80,8,128]{2,1,0:T(8,128)} %constant.2.clone.tab_ref, s32[1,128]{1,0:T(1,128)} %bitcast.1, f32[3]{0:T(128)} %kap_ref.1), custom_call_target="tpu_custom_call" | custom-call | tf_op jit(solution)/shard_map/pallas_call | solution.py:372
  46.0 3.8 %shard_map.87 = (f32[3,512,128]{2,1,0:T(8,128)}, f32[3,512,128]{2,1,0:T(8,128)}) custom-call(s32[1,128]{1,0:T(1,128)} %bitcast.2, f32[3,512,128]{2,1,0:T(8,128)} %get-tuple-element.4.f_ref, f32[3,512,128]{2,1,0:T(8,128)} %get-tuple-element.5.a_ref), custom_call_target="tpu_custom_call" | custom-call | tf_op jit(solution)/shard_map/pallas_call | solution.py:338

commit v12 on v10

--- a/solution.py
+++ b/solution.py
@@ -323,23 +323,43 @@
         out_f_in[f] = out_f_ref[f].reshape(512, 128)
 
 
-def unsort_kernel(num_ref, f_ref, a_ref, out_f, out_a):
+def unsort_kernel(num_ref, f_hbm, a_hbm, out_f, out_a, buf_in, buf_out, sem_in, sem_out):
     count = num_ref.shape[1]
+    fields = f_hbm.shape[0]
+    srcs = [r.at[f] for f in range(fields) for r in (f_hbm, a_hbm)]
+    dsts = [r.at[f] for f in range(fields) for r in (out_f, out_a)]
+    loads = [pltpu.make_async_copy(s, buf_in.at[i], sem_in.at[i]) for i, s in enumerate(srcs)]
+    for c in loads:
+        c.start()
     height = lax.rem(num_ref[...], count)
     p_out = (lax.broadcasted_iota(jnp.int32, (count, count), 0) == height).astype(jnp.bfloat16)
-    for f in range(f_ref.shape[0]):
-        out_f[f] = permute(f_ref[f], p_out, False)
-        out_a[f] = permute(a_ref[f], p_out, False)
+    stores = []
+    for i, c in enumerate(loads):
+        c.wait()
+        buf_out[i] = permute(buf_in[i], p_out, False)
+        st = pltpu.make_async_copy(buf_out.at[i], dsts[i], sem_out.at[i])
+        st.start()
+        stores.append(st)
+    for st in stores:
+        st.wait()
 
 
 def unsort(numbering, moments, sensitivities):
     vmem = pl.BlockSpec(memory_space=pltpu.VMEM)
+    hbm = pl.BlockSpec(memory_space=pl.ANY)
+    slabs = 2 * moments.shape[0]
     shape = jax.ShapeDtypeStruct(moments.shape, jnp.float32)
     return pl.pallas_call(
         unsort_kernel,
         out_shape=(shape, shape),
-        in_specs=[vmem, vmem, vmem],
-        out_specs=(vmem, vmem),
+        in_specs=[vmem, hbm, hbm],
+        out_specs=(hbm, hbm),
+        scratch_shapes=[
+            pltpu.VMEM((slabs,) + moments.shape[1:], jnp.float32),
+            pltpu.VMEM((slabs,) + moments.shape[1:], jnp.float32),
+            pltpu.SemaphoreType.DMA((slabs,)),
+            pltpu.SemaphoreType.DMA((slabs,)),
+        ],
     )(numbering, moments, sensitivities)
 
 

time: 49.5 us -> 50.7 us (1.024)
  Pallas kernels: 48.7 us -> 49.8 us
    pallas_call x1, Pallas kernels: 3.3 us -> 4.43 us  [unsort(): pl.pallas_call(unsort_kernel, out_shape=(shape, shape), in_specs=[vmem, h...]
where the time goes in v12:
time: 50.7 us; the launch traced here: 50.6 us
  Pallas kernels  49.8 us (98%)
  between operations  0.8 us (2%)
    pallas_call x1, Pallas kernels, fused(): pl.pallas_call(functools.partial(kernel, ndev, cols), out_shape=(jax.Shap...  45.4 us
    pallas_call x1, Pallas kernels, unsort(): pl.pallas_call(unsort_kernel, out_shape=(shape, shape), in_specs=[vmem, h...  4.43 us

profile of v12, /device:TPU:63, one launch (start us, length us, event | category | flops | bytes accessed | tf_op | source)
XLA Modules:
  0.0 50.6 jit_solution(2646960733594288441)
XLA Ops:
  0.6 45.4 %shard_map.86 = (f32[3,512,128]{2,1,0:T(8,128)}, f32[3,512,128]{2,1,0:T(8,128)}) custom-call(f32[3,512,128]{2,1,0:T(8,128)} %fld_in.1, f32[3,512,128]{2,1,0:T(8,128)} %adj_in.1, f32[3,512,128]{2,1,0:T(8,128)} %vel_in.1, f32[512,128]{1,0:T(8,128)} %mass_in.1, f32[80,8,128]{2,1,0:T(8,128)} %constant.2.clone.tab_ref, s32[1,128]{1,0:T(1,128)} %bitcast.1, f32[3]{0:T(128)} %kap_ref.1), custom_call_target="tpu_custom_call" | custom-call | tf_op jit(solution)/shard_map/pallas_call | solution.py:391
  46.0 4.4 %shard_map.87 = (f32[3,512,128]{2,1,0:T(8,128)}, f32[3,512,128]{2,1,0:T(8,128)}) custom-call(s32[1,128]{1,0:T(1,128)} %bitcast.2, f32[3,512,128]{2,1,0:T(8,128)} %get-tuple-element.4.f_hbm, f32[3,512,128]{2,1,0:T(8,128)} %get-tuple-element.5.a_hbm), custom_call_target="tpu_custom_call" | custom-call | tf_op jit(solution)/shard_map/pallas_call | solution.py:352

commit v13 on v10

--- a/solution.py
+++ b/solution.py
@@ -183,6 +183,7 @@
     rd,
     ssem,
     rsem,
+    osem,
 ):
     me = lax.axis_index("elem")
     column = (me + cols // 2) % ndev
@@ -313,14 +314,19 @@
         f1_ref[f] = f1
         xs[10 + f] = forward_terms(f1, flow(), mass_ref[...], kap_ref[f], tab_ref)
         start_group(7 + f)
+    outs = []
     for f in range(3):
         finish_group(4 + f)
         out_a_ref[f] = a1_ref[f] + time_step * adjoint_terms(xs[7 + f], flow(), mass_ref[...], kap_ref[f], tab_ref)
-        out_a_in[f] = out_a_ref[f].reshape(512, 128)
+        outs.append(pltpu.make_async_copy(out_a_ref.at[f], out_a_in.at[f], osem.at[f]))
+        outs[-1].start()
     for f in range(3):
         finish_group(7 + f)
         out_f_ref[f] = f1_ref[f] + time_step * xs[10 + f] / ms_ref[...]
-        out_f_in[f] = out_f_ref[f].reshape(512, 128)
+        outs.append(pltpu.make_async_copy(out_f_ref.at[f], out_f_in.at[f], osem.at[3 + f]))
+        outs[-1].start()
+    for c in outs:
+        c.wait()
 
 
 def unsort_kernel(num_ref, f_ref, a_ref, out_f, out_a):
@@ -367,12 +373,13 @@
     for _ in range(2):
         scratch.append(pltpu.VMEM((groups, 4, 4, 8, 128), f32))
     scratch += [pltpu.SemaphoreType.DMA((groups, 8)), pltpu.SemaphoreType.DMA((groups, 8))]
+    scratch.append(pltpu.SemaphoreType.DMA((6,)))
     shape = fields.shape
     return pl.pallas_call(
         functools.partial(kernel, ndev, cols),
-        out_shape=(jax.ShapeDtypeStruct(shape, f32), jax.ShapeDtypeStruct(shape, f32)),
+        out_shape=(jax.ShapeDtypeStruct((3,) + cube, f32), jax.ShapeDtypeStruct((3,) + cube, f32)),
         in_specs=[vmem, vmem, vmem, vmem, vmem, vmem, smem],
-        out_specs=(vmem, vmem),
+        out_specs=(pl.BlockSpec(memory_space=pl.ANY), pl.BlockSpec(memory_space=pl.ANY)),
         scratch_shapes=scratch,
         compiler_params=pltpu.CompilerParams(
             collective_id=0, has_side_effects=True, vmem_limit_bytes=60 * 1024 * 1024
@@ -389,7 +396,8 @@
         moment_fields, adjoint_fields, velocity, mass_weights, table,
         row_numbers, diffusivity, ndev, cols,
     )
-    return unsort(row_numbers, moments, sensitivities)
+    shape = moment_fields.shape
+    return unsort(row_numbers, moments.reshape(shape), sensitivities.reshape(shape))
 
 
 def solution(mesh):

time: 49.5 us -> 49.1 us (level)
  no operation moved by 1% of the time
where the time goes in v13:
time: 49.1 us; the launch traced here: 48.9 us
  Pallas kernels  48.3 us (98%)
  between operations  0.64 us (1%)
    pallas_call x1, Pallas kernels, fused(): pl.pallas_call(functools.partial(kernel, ndev, cols), out_shape=(jax.Shap...  45 us
    pallas_call x1, Pallas kernels, unsort(): pl.pallas_call(unsort_kernel, out_shape=(shape, shape), in_specs=[vmem, v...  3.3 us

profile of v13, /device:TPU:63, one launch (start us, length us, event | category | flops | bytes accessed | tf_op | source)
XLA Modules:
  0.0 48.9 jit_solution(17061529293606467743)
XLA Ops:
  0.6 45.0 %shard_map.86 = (f32[3,8,8,8,128]{4,3,2,1,0:T(8,128)}, f32[3,8,8,8,128]{4,3,2,1,0:T(8,128)}) custom-call(f32[3,512,128]{2,1,0:T(8,128)} %fld_in.1, f32[3,512,128]{2,1,0:T(8,128)} %adj_in.1, f32[3,512,128]{2,1,0:T(8,128)} %vel_in.1, f32[512,128]{1,0:T(8,128)} %mass_in.1, f32[80,8,128]{2,1,0:T(8,128)} %constant.2.clone.tab_ref, s32[1,128]{1,0:T(1,128)} %bitcast.5, ...), custom_call_target="tpu_custom_call" | custom-call | tf_op jit(solution)/shard_map/pallas_call | solution.py:378
  45.6 3.3 %shard_map.87 = (f32[3,512,128]{2,1,0:T(8,128)}, f32[3,512,128]{2,1,0:T(8,128)}) custom-call(s32[1,128]{1,0:T(1,128)} %bitcast.6, f32[3,512,128]{2,1,0:T(8,128)} %bitcast.3, f32[3,512,128]{2,1,0:T(8,128)} %bitcast.4), custom_call_target="tpu_custom_call" | custom-call | tf_op jit(solution)/shard_map/pallas_call | solution.py:344
